TPU v7x, 32 devices: a whole 2x2x4 slice. The times are simulated.
32 devices in a mesh: fsdp: 8 (over y, x, core), tensor: 4 (over z).
Axes of the slice: x: 2, y: 2, z: 4, core: 2. Of those that a mesh axis runs over, the one named last changes fastest.
Arguments:
- tokens: bfloat16 [4096, 1152], P(('fsdp', 'tensor')), may hold values from -6 to 6
- cotangent: bfloat16 [4096, 1152], P(('fsdp', 'tensor')), may hold values from -6 to 6
- first_gain: float32 [1152], replicated, may hold values from 0.5 to 1.5
- first_shift: float32 [1152], replicated, may hold values from -1.5 to 1.5
- query_weight: bfloat16 [1152, 1152], P('fsdp', 'tensor'), may hold values from -2 to 2
- key_weight: bfloat16 [1152, 1152], P('fsdp', 'tensor'), may hold values from -2 to 2
- value_weight: bfloat16 [1152, 1152], P('fsdp', 'tensor'), may hold values from -0.1875 to 0.1875
- query_bias: float32 [1152], P('tensor'), may hold values from -2.5 to 2.5
- value_bias: float32 [1152], P('tensor'), may hold values from -2.5 to 2.5
- out_weight: bfloat16 [1152, 1152], P('tensor', 'fsdp'), may hold values from -1.5 to 1.5
- out_bias: float32 [1152], replicated, may hold values from -2.5 to 2.5
- second_gain: float32 [1152], replicated, may hold values from 0.5 to 1.5
- second_shift: float32 [1152], replicated, may hold values from -1.5 to 1.5
- up_weight: bfloat16 [1152, 4304], P('fsdp', 'tensor'), may hold values from -0.1875 to 0.1875
- up_bias: float32 [4304], P('tensor'), may hold values from -2.5 to 2.5
- down_weight: bfloat16 [4304, 1152], P('tensor', 'fsdp'), may hold values from -0.09375 to 0.09375
- down_bias: float32 [1152], replicated, may hold values from -2.5 to 2.5
Outputs:
- layer_out: bfloat16 [4096, 1152], P(('fsdp', 'tensor'))
- input_grad: float32 [4096, 1152], P(('fsdp', 'tensor'))
- first_gain_gradient: float32 [1152], replicated
- first_shift_gradient: float32 [1152], replicated
- query_weight_gradient: float32 [1152, 1152], P('fsdp', 'tensor')
- key_weight_gradient: float32 [1152, 1152], P('fsdp', 'tensor')
- value_weight_gradient: float32 [1152, 1152], P('fsdp', 'tensor')
- query_bias_gradient: float32 [1152], P('tensor')
- value_bias_gradient: float32 [1152], P('tensor')
- out_weight_gradient: float32 [1152, 1152], P('tensor', 'fsdp')
- out_bias_gradient: float32 [1152], replicated
- second_gain_gradient: float32 [1152], replicated
- second_shift_gradient: float32 [1152], replicated
- up_weight_gradient: float32 [1152, 4304], P('fsdp', 'tensor')
- up_bias_gradient: float32 [4304], P('tensor')
- down_weight_gradient: float32 [4304, 1152], P('tensor', 'fsdp')
- down_bias_gradient: float32 [1152], replicated
All inputs are finite; a program needn't handle non-finite values.
Results may differ from a plain program's by a relative error of at most 0.014.
Values may be sent and summed in bfloat16 or wider, within the bound.
A program may use at most 128 MiB of HBM per device.

v0:
```python
import math

import jax
import jax.numpy as jnp
from jax import lax
from jax.sharding import PartitionSpec as P

D = 1152
HD = 72
FF = 4304
SEQ = 256


norm_eps = 1e-06
gelu_coef = 0.7978845608028654
cubic_coef = 0.044715


def dot_plain(left, right):
    return jnp.dot(left, right, preferred_element_type=jnp.float32)


def dot_right_t(left, right):
    return lax.dot_general(
        left, right, (((1,), (1,)), ((), ())), preferred_element_type=jnp.float32
    )


def dot_left_t(left, right):
    return lax.dot_general(
        left, right, (((0,), (0,)), ((), ())), preferred_element_type=jnp.float32
    )


def norm_rows(values, gain, shift):
    row_mean = jnp.mean(values, axis=1, keepdims=True)
    centred = values - row_mean
    inv_scale = lax.rsqrt(jnp.mean(centred * centred, axis=1, keepdims=True) + norm_eps)
    normed = centred * inv_scale
    return (normed * gain + shift, normed, inv_scale)


def norm_back(out_grad, normed, inv_scale, gain):
    scaled_grad = out_grad * gain
    grad_mean = jnp.mean(scaled_grad, axis=1, keepdims=True)
    cross_mean = jnp.mean(scaled_grad * normed, axis=1, keepdims=True)
    in_grad = inv_scale * (scaled_grad - grad_mean - normed * cross_mean)
    return (in_grad, jnp.sum(out_grad * normed, axis=0), jnp.sum(out_grad, axis=0))


def gelu_pair(upper):
    tangent = jnp.tanh(gelu_coef * (upper + cubic_coef * upper * upper * upper))
    gelu_value = 0.5 * upper * (1.0 + tangent)
    gelu_slope = 0.5 * (1.0 + tangent) + 0.5 * upper * (1.0 - tangent * tangent) * gelu_coef * (
        1.0 + 3.0 * cubic_coef * upper * upper
    )
    return (gelu_value, gelu_slope)


def split_heads(block_rows, head_count):
    col_width = block_rows.shape[1] // 3
    img_count = block_rows.shape[0] // SEQ
    shape_four = (img_count, SEQ, head_count, HD)
    queries = block_rows[:, :col_width].reshape(shape_four)
    keys_part = block_rows[:, col_width : 2 * col_width].reshape(shape_four)
    values = block_rows[:, 2 * col_width :].reshape(shape_four)
    return (queries, keys_part, values, shape_four)


def attend_forward(block_rows, head_count):
    queries, keys_part, values, shape_four = split_heads(block_rows, head_count)
    scores = jnp.einsum(
        "nqhd,nkhd->nhqk", queries, keys_part, preferred_element_type=jnp.float32
    ) * HD ** (-0.5)
    peak = jnp.max(scores, axis=-1, keepdims=True)
    expo = jnp.exp(scores - peak)
    totals = jnp.sum(expo, axis=-1, keepdims=True)
    prob_low = (expo / totals).astype(jnp.bfloat16)
    mixed = jnp.einsum("nhqk,nkhd->nqhd", prob_low, values, preferred_element_type=jnp.float32)
    row_total = block_rows.shape[0]
    mixed = mixed.reshape(row_total, head_count * HD).astype(jnp.bfloat16)
    return (mixed, (peak + jnp.log(totals))[..., 0])


def attend_backward(inputs, head_count):
    block_rows, grad_block, log_total = inputs
    queries, keys_part, values, shape_four = split_heads(block_rows, head_count)
    grad_out = grad_block.reshape(shape_four)
    scores = jnp.einsum(
        "nqhd,nkhd->nhqk", queries, keys_part, preferred_element_type=jnp.float32
    ) * HD ** (-0.5)
    probs = jnp.exp(scores - log_total[..., None])
    prob_low = probs.astype(jnp.bfloat16)
    value_grad = jnp.einsum(
        "nhqk,nqhd->nkhd", prob_low, grad_out, preferred_element_type=jnp.float32
    )
    prob_grad = jnp.einsum("nqhd,nkhd->nhqk", grad_out, values, preferred_element_type=jnp.float32)
    row_dot = jnp.sum(probs * prob_grad, axis=-1, keepdims=True)
    score_grad = (probs * (prob_grad - row_dot)).astype(jnp.bfloat16)
    query_grad = jnp.einsum(
        "nhqk,nkhd->nqhd", score_grad, keys_part, preferred_element_type=jnp.float32
    ) * HD ** (-0.5)
    key_grad = jnp.einsum(
        "nhqk,nqhd->nkhd", score_grad, queries, preferred_element_type=jnp.float32
    ) * HD ** (-0.5)
    row_total = block_rows.shape[0]
    col_width = head_count * HD
    return jnp.concatenate(
        (
            query_grad.reshape(row_total, col_width),
            key_grad.reshape(row_total, col_width),
            value_grad.reshape(row_total, col_width),
        ),
        axis=1,
    ).astype(jnp.bfloat16)


def on_device(
    tokens,
    cotangent,
    first_gain,
    first_shift,
    query_weight,
    key_weight,
    value_weight,
    query_bias,
    value_bias,
    out_weight,
    out_bias,
    second_gain,
    second_shift,
    up_weight,
    up_bias,
    down_weight,
    down_bias,
):
    full_query, full_key, full_value, full_outp, full_up, full_down = (
        lax.all_gather(query_weight, "fsdp", axis=0, tiled=True),
        lax.all_gather(key_weight, "fsdp", axis=0, tiled=True),
        lax.all_gather(value_weight, "fsdp", axis=0, tiled=True),
        lax.all_gather(out_weight, "fsdp", axis=1, tiled=True),
        lax.all_gather(up_weight, "fsdp", axis=0, tiled=True),
        lax.all_gather(down_weight, "fsdp", axis=1, tiled=True),
    )
    qkv_weight = jnp.concatenate((full_query, full_key, full_value), axis=1)
    local_width = full_query.shape[1]
    ffn_width = full_up.shape[1]
    head_count = local_width // HD
    token_rows = tokens.astype(jnp.float32)
    first_out, first_hat, first_scale = norm_rows(token_rows, first_gain, first_shift)
    all_first = lax.all_gather(first_out.astype(jnp.bfloat16), "tensor", axis=0, tiled=True)
    qkv_bias = jnp.concatenate((query_bias, jnp.zeros_like(query_bias), value_bias))
    qkv_rows = (dot_plain(all_first, qkv_weight) + qkv_bias).astype(jnp.bfloat16)
    group_rows = qkv_rows.shape[0]
    images = group_rows // SEQ
    per_block = math.gcd(images, max(1, 512 // SEQ))
    blocks = images // per_block
    stacked = qkv_rows.reshape(blocks, per_block * SEQ, 3 * local_width)

    def forward_block(block_rows):
        return attend_forward(block_rows, head_count)

    head_out, log_total = lax.map(forward_block, stacked)
    head_out = head_out.reshape(group_rows, local_width)
    attn_rows = lax.psum_scatter(
        dot_plain(head_out, full_outp), "tensor", scatter_dimension=0, tiled=True
    )
    mid_rows = token_rows + attn_rows + out_bias
    second_out, second_hat, second_scale = norm_rows(mid_rows, second_gain, second_shift)
    all_second = lax.all_gather(second_out.astype(jnp.bfloat16), "tensor", axis=0, tiled=True)
    up_pre = dot_plain(all_second, full_up) + up_bias
    hidden_value, hidden_slope = gelu_pair(up_pre)
    hidden_low = hidden_value.astype(jnp.bfloat16)
    mlp_rows = lax.psum_scatter(
        dot_plain(hidden_low, full_down).astype(jnp.bfloat16),
        "tensor",
        scatter_dimension=0,
        tiled=True,
    ).astype(jnp.float32)
    layer_out = (mid_rows + mlp_rows + down_bias).astype(jnp.bfloat16)
    out_grad = cotangent.astype(jnp.float32)
    all_out_grad = lax.all_gather(cotangent, "tensor", axis=0, tiled=True)
    down_grad = dot_left_t(hidden_low, all_out_grad)
    hidden_grad = dot_right_t(all_out_grad, full_down)
    upper_low = (hidden_grad * hidden_slope).astype(jnp.bfloat16)
    up_bias_grad = jnp.sum(upper_low.astype(jnp.float32), axis=0)
    up_grad = dot_left_t(all_second, upper_low)
    second_grad = lax.psum_scatter(
        dot_right_t(upper_low, full_up), "tensor", scatter_dimension=0, tiled=True
    )
    back_second, second_gain_grad, second_shift_grad = norm_back(
        second_grad, second_hat, second_scale, second_gain
    )
    mid_grad = out_grad + back_second
    mid_low = mid_grad.astype(jnp.bfloat16)
    all_mid_grad = lax.all_gather(mid_low, "tensor", axis=0, tiled=True)
    outp_grad = dot_left_t(head_out, all_mid_grad)
    head_grad = dot_right_t(all_mid_grad, full_outp).astype(jnp.bfloat16)

    def backward_block(inputs):
        return attend_backward(inputs, head_count)

    qkv_grad = lax.map(
        backward_block,
        (stacked, head_grad.reshape(blocks, per_block * SEQ, local_width), log_total),
    )
    qkv_grad = qkv_grad.reshape(group_rows, 3 * local_width)
    qkv_weight_grad = dot_left_t(all_first, qkv_grad)
    qkv_bias_grad = jnp.sum(qkv_grad.astype(jnp.float32), axis=0)
    first_grad = lax.psum_scatter(
        dot_right_t(qkv_grad, qkv_weight).astype(jnp.bfloat16),
        "tensor",
        scatter_dimension=0,
        tiled=True,
    ).astype(jnp.float32)
    back_first, first_gain_grad, first_shift_grad = norm_back(
        first_grad, first_hat, first_scale, first_gain
    )
    input_grad = mid_grad + back_first
    out_bias_grad = jnp.sum(mid_low.astype(jnp.float32), axis=0)
    down_bias_grad = jnp.sum(out_grad, axis=0)
    small_terms = jnp.concatenate(
        (
            first_gain_grad,
            first_shift_grad,
            out_bias_grad,
            second_gain_grad,
            second_shift_grad,
            down_bias_grad,
        )
    )
    tensor_index = lax.axis_index("tensor")
    head_terms = jnp.zeros((2 * D + FF,), jnp.float32)
    head_terms = lax.dynamic_update_slice(
        head_terms, qkv_bias_grad[:local_width], (tensor_index * local_width,)
    )
    head_terms = lax.dynamic_update_slice(
        head_terms, qkv_bias_grad[2 * local_width :], (D + tensor_index * local_width,)
    )
    head_terms = lax.dynamic_update_slice(
        head_terms, up_bias_grad, (2 * D + tensor_index * ffn_width,)
    )
    small_sums, head_sums = lax.psum((small_terms, head_terms), ("fsdp", "tensor"))
    query_bias_total = lax.dynamic_slice(head_sums, (tensor_index * local_width,), (local_width,))
    value_bias_total = lax.dynamic_slice(
        head_sums, (D + tensor_index * local_width,), (local_width,)
    )
    up_bias_total = lax.dynamic_slice(head_sums, (2 * D + tensor_index * ffn_width,), (ffn_width,))
    query_part, key_part, value_part, outp_part, up_part, down_part = (
        lax.psum_scatter(qkv_weight_grad[:, :local_width], "fsdp", scatter_dimension=0, tiled=True),
        lax.psum_scatter(
            qkv_weight_grad[:, local_width : 2 * local_width],
            "fsdp",
            scatter_dimension=0,
            tiled=True,
        ),
        lax.psum_scatter(
            qkv_weight_grad[:, 2 * local_width :], "fsdp", scatter_dimension=0, tiled=True
        ),
        lax.psum_scatter(outp_grad, "fsdp", scatter_dimension=1, tiled=True),
        lax.psum_scatter(up_grad, "fsdp", scatter_dimension=0, tiled=True),
        lax.psum_scatter(down_grad, "fsdp", scatter_dimension=1, tiled=True),
    )
    return (
        layer_out,
        input_grad,
        small_sums[0:D],
        small_sums[D : 2 * D],
        query_part,
        key_part,
        value_part,
        query_bias_total,
        value_bias_total,
        outp_part,
        small_sums[2 * D : 3 * D],
        small_sums[3 * D : 4 * D],
        small_sums[4 * D : 5 * D],
        up_part,
        up_bias_total,
        down_part,
        small_sums[5 * D : 6 * D],
    )


def solution(mesh):
    return jax.shard_map(
        on_device,
        mesh=mesh,
        in_specs=(
            P(("fsdp", "tensor"), None),
            P(("fsdp", "tensor"), None),
            P(),
            P(),
            P("fsdp", "tensor"),
            P("fsdp", "tensor"),
            P("fsdp", "tensor"),
            P("tensor"),
            P("tensor"),
            P("tensor", "fsdp"),
            P(),
            P(),
            P(),
            P("fsdp", "tensor"),
            P("tensor"),
            P("tensor", "fsdp"),
            P(),
        ),
        out_specs=(
            P(("fsdp", "tensor"), None),
            P(("fsdp", "tensor"), None),
            P(),
            P(),
            P("fsdp", "tensor"),
            P("fsdp", "tensor"),
            P("fsdp", "tensor"),
            P("tensor"),
            P("tensor"),
            P("tensor", "fsdp"),
            P(),
            P(),
            P(),
            P("fsdp", "tensor"),
            P("tensor"),
            P("tensor", "fsdp"),
            P(),
        ),
        check_vma=False,
    )
```

profile of v0, /device:TPU:1, one launch (start us, length us, event | category | flops | bytes accessed | tf_op | source)
XLA Modules:
  0.0 676.8 jit_solution(887456628417421847)
XLA Ops:
  8.1 1.1 convert_reduce_fusion.3
  9.2 1.2 fusion.29
  10.5 1.9 fusion.25
  13.3 14.0 %all_gather.31 = bf16[1152,288]{1,0:T(8,128)(2,1)} all-gather(bf16[144,288]{1,0:T(8,128)(2,1)} %param.21), channel_id=1, replica_groups=mesh['fsdp'=8,'tensor'=4] {'fsdp'}, dimensions={0}, use_global_device_ids=true | all-gather | bytes 746496 | tf_op jit(solution)/shard_map/all_gather | solution.py:138
  27.2 11.3 %all_gather.32 = bf16[1152,288]{1,0:T(8,128)(2,1)} all-gather(bf16[144,288]{1,0:T(8,128)(2,1)S(1)} %copy-done.15), channel_id=1, replica_groups=mesh['fsdp'=8,'tensor'=4] {'fsdp'}, dimensions={0}, use_global_device_ids=true | all-gather | bytes 746496 | tf_op jit(solution)/shard_map/all_gather | solution.py:139
  38.6 11.3 %all_gather.33 = bf16[1152,288]{1,0:T(8,128)(2,1)} all-gather(bf16[144,288]{1,0:T(8,128)(2,1)S(1)} %copy-done.16), channel_id=1, replica_groups=mesh['fsdp'=8,'tensor'=4] {'fsdp'}, dimensions={0}, use_global_device_ids=true | all-gather | bytes 746496 | tf_op jit(solution)/shard_map/all_gather | solution.py:140
  49.9 10.1 %all_gather.34 = bf16[288,1152]{0,1:T(8,128)(2,1)S(1)} all-gather(bf16[288,144]{0,1:T(8,128)(2,1)S(1)} %copy-done.17), channel_id=1, replica_groups=mesh['fsdp'=8,'tensor'=4] {'fsdp'}, dimensions={1}, use_global_device_ids=true | all-gather | bytes 746496 | tf_op jit(solution)/shard_map/all_gather | solution.py:141
  60.0 4.7 add_convert_fusion
  65.6 0.8 reshape.150
  66.4 1.5 multiply_reduce_fusion.1
  69.9 2.3 fusion.54
  72.9 47.2 %reduce-scatter.17.cloned.1.call-done = f32[128,1152]{1,0:T(8,128)} async-done(((f32[512,1152]{1,0:T(8,128)}), f32[128,1152]{1,0:T(8,128)}) %reduce-scatter.17.cloned.1.call-update) | async-done | bytes 589840 | tf_op jit(solution)/shard_map/reduce_scatter | solution.py:165
  120.1 1.2 fusion.48
  121.6 0.9 add_convert_fusion.2
  124.1 27.8 %all-gather.9.cloned.1.call-done = bf16[512,1152]{1,0:T(8,128)(2,1)} async-done(((bf16[128,1152]{1,0:T(8,128)(2,1)}), bf16[512,1152]{1,0:T(8,128)(2,1)}) %all-gather.9.cloned.1.call-update) | async-done | bytes 1179664 | tf_op jit(solution)/shard_map/all_gather | solution.py:170
  151.9 5.1 convolution_add_fusion
  157.0 25.7 %all-gather.15.cloned.1.call-done = bf16[512,1152]{1,0:T(8,128)(2,1)} async-done(((bf16[128,1152]{1,0:T(8,128)(2,1)}), bf16[512,1152]{1,0:T(8,128)(2,1)}) %all-gather.15.cloned.1.call-update) | async-done | bytes 1179664 | tf_op jit(solution)/shard_map/all_gather | solution.py:182
  182.8 32.2 %all-gather.13.cloned.1.call-done = bf16[1076,1152]{0,1:T(8,128)(2,1)} async-done(((bf16[1076,144]{0,1:T(8,128)(2,1)}), bf16[1076,1152]{0,1:T(8,128)(2,1)}) %all-gather.13.cloned.1.call-update) | async-done | bytes 2479120 | tf_op jit(solution)/shard_map/all_gather | solution.py:143
  215.0 5.8 convert_reduce_fusion
  220.8 1.0 copy-done.27
  221.8 3.3 fusion.55
  225.2 5.8 convolution_convert_fusion.1
  231.0 41.7 %reduce-scatter.21.cloned.1.call-done = f32[128,1152]{1,0:T(8,128)} async-done(((f32[512,1152]{1,0:T(8,128)}), f32[128,1152]{1,0:T(8,128)}) %reduce-scatter.21.cloned.1.call-update) | async-done | bytes 589840 | tf_op jit(solution)/shard_map/reduce_scatter | solution.py:188
  272.7 1.3 multiply_reduce_fusion.2
  274.1 29.5 %reduce-scatter.19.cloned.1.call-done = bf16[128,1152]{1,0:T(8,128)(2,1)} async-done(((bf16[512,1152]{1,0:T(8,128)(2,1)}), bf16[128,1152]{1,0:T(8,128)(2,1)}) %reduce-scatter.19.cloned.1.call-update) | async-done | bytes 294928 | tf_op jit(solution)/shard_map/reduce_scatter | solution.py:174
  303.6 2.5 convert_reduce_fusion.5
  306.4 28.3 %all-gather.17.cloned.1.call-done = bf16[512,1152]{1,0:T(8,128)(2,1)} async-done(((bf16[128,1152]{1,0:T(8,128)(2,1)}), bf16[512,1152]{1,0:T(8,128)(2,1)}) %all-gather.17.cloned.1.call-update) | async-done | bytes 1179664 | tf_op jit(solution)/shard_map/all_gather | solution.py:196
  334.7 2.1 convolution_convert_fusion.2
  342.3 3.2 convolution_convert_fusion
  345.5 5.8 fusion.47
  351.4 1.3 copy-done.24
  352.7 5.3 fusion.57
  358.1 1.2 copy-done.2
  359.3 2.0 fusion.56
  361.7 2.6 fusion.58
  364.3 1.7 fusion.50
  366.0 3.1 copy.95
  369.3 3.1 copy.93
  372.4 1.8 copy.91
  375.1 1.3 fusion.32
  376.4 41.4 %all-reduce = (f32[6912]{0:T(1024)S(1)}, f32[6608]{0:T(1024)S(1)}) all-reduce(f32[6912]{0:T(1024)S(1)} %constant_dynamic-update-slice_fusion.4, f32[6608]{0:T(1024)S(1)} %dynamic_update_slice.20), channel_id=1, replica_groups=mesh['fsdp'=8,'tensor'=4] {'fsdp','tensor'}, use_global_device_ids=true, to_apply=%region_21.22 | all-reduce | flops 13520 | bytes 108160 | tf_op jit(solution)/shard_map/psum | solution.py:243
  419.8 2.0 fusion.28
  421.8 13.0 %reduce-scatter.29.cloned.1.call-done = f32[1076,144]{0,1:T(8,128)} async-done(((f32[1076,1152]{0,1:T(8,128)}), f32[1076,144]{0,1:T(8,128)}) %reduce-scatter.29.cloned.1.call-update) | async-done | bytes 619792 | tf_op jit(solution)/shard_map/reduce_scatter | solution.py:262
  434.8 61.3 %reduce-scatter.27.cloned.1.call-done = f32[144,1076]{1,0:T(8,128)} async-done(((f32[1152,1076]{1,0:T(8,128)}), f32[144,1076]{1,0:T(8,128)}) %reduce-scatter.27.cloned.1.call-update) | async-done | bytes 619792 | tf_op jit(solution)/shard_map/reduce_scatter | solution.py:261
  496.2 43.4 %reduce-scatter.25.cloned.1.call-done = f32[288,144]{0,1:T(8,128)} async-done(((f32[288,1152]{0,1:T(8,128)}), f32[288,144]{0,1:T(8,128)}) %reduce-scatter.25.cloned.1.call-update) | async-done | bytes 165904 | tf_op jit(solution)/shard_map/reduce_scatter | solution.py:260
  539.5 43.4 %reduce-scatter.35.cloned.1.call-done = f32[144,288]{1,0:T(8,128)} async-done(((f32[1152,288]{1,0:T(8,128)}), f32[144,288]{1,0:T(8,128)}) %reduce-scatter.35.cloned.1.call-update) | async-done | bytes 165904
  582.9 43.2 %reduce-scatter.33.cloned.1.call-done = f32[144,288]{1,0:T(8,128)} async-done(((f32[1152,288]{1,0:T(8,128)}), f32[144,288]{1,0:T(8,128)}) %reduce-scatter.33.cloned.1.call-update) | async-done | bytes 165904
  626.1 43.4 %reduce-scatter.31.cloned.1.call-done = f32[144,288]{1,0:T(8,128)} async-done(((f32[1152,288]{1,0:T(8,128)}), f32[144,288]{1,0:T(8,128)}) %reduce-scatter.31.cloned.1.call-update) | async-done | bytes 165904
  (136 shorter events, 15.4 us)
Async XLA Ops:
  8.0 19.2 %copy-start.15 = (bf16[144,288]{1,0:T(8,128)(2,1)S(1)}, bf16[144,288]{1,0:T(8,128)(2,1)}, u32[]{:S(2)}) copy-start(bf16[144,288]{1,0:T(8,128)(2,1)} %param.22) | copy-start | bytes 248836
  8.0 30.5 %copy-start.16 = (bf16[144,288]{1,0:T(8,128)(2,1)S(1)}, bf16[144,288]{1,0:T(8,128)(2,1)}, u32[]{:S(2)}) copy-start(bf16[144,288]{1,0:T(8,128)(2,1)} %param.23) | copy-start | bytes 248836
  8.0 51.9 %all-gather.7.cloned.1.call-start = ((), (), s32[]{:S(2)}) async-start(), calls=%async_computation.10 | async-start | bytes 1474560 | tf_op jit(solution)/shard_map/all_gather | solution.py:151
  9.2 40.6 %copy-start.17 = (bf16[288,144]{0,1:T(8,128)(2,1)S(1)}, bf16[288,144]{0,1:T(8,128)(2,1)}, u32[]{:S(2)}) copy-start(bf16[288,144]{0,1:T(8,128)(2,1)} %param.26) | copy-start | bytes 248836
  12.4 107.7 %reduce-scatter.17.cloned.1.call-start = ((), (), s32[]{:S(2)}) async-start(), calls=%async_computation.11 | async-start | bytes 2949120 | tf_op jit(solution)/shard_map/reduce_scatter | solution.py:165
  60.0 9.3 %copy-start.1 = (bf16[288,1152]{0,1:T(8,128)(2,1)}, bf16[288,1152]{0,1:T(8,128)(2,1)S(1)}, u32[]{:S(2)}) copy-start(bf16[288,1152]{0,1:T(8,128)(2,1)S(1)} %all_gather.34) | copy-start | bytes 1990660
  65.6 2.7 copy-start.5
  66.4 1.9 copy-start.10
  69.2 0.7 copy-start.3
  72.2 47.9 %copy-start = (bf16[128,1152]{1,0:T(8,128)(2,1)S(1)}, bf16[128,1152]{1,0:T(8,128)(2,1)}, u32[]{:S(2)}) copy-start(bf16[128,1152]{1,0:T(8,128)(2,1)} %param.17) | copy-start | bytes 884740
  72.2 47.9 %copy-start.20 = (f32[1152]{0:T(1024)S(1)}, f32[1152]{0:T(1024)}, u32[]{:S(2)}) copy-start(f32[1152]{0:T(1024)} %param.27) | copy-start | bytes 13828
  72.2 49.3 %copy-start.18 = (f32[1152]{0:T(1024)S(1)}, f32[1152]{0:T(1024)}, u32[]{:S(2)}) copy-start(f32[1152]{0:T(1024)} %param.28) | copy-start | bytes 13828
  72.2 49.4 %copy-start.21 = (f32[1152]{0:T(1024)S(1)}, f32[1152]{0:T(1024)}, u32[]{:S(2)}) copy-start(f32[1152]{0:T(1024)} %param.29) | copy-start | bytes 13828
  72.2 79.6 %copy-start.26 = (f32[1076]{0:T(1024)S(1)}, f32[1076]{0:T(1024)}, u32[]{:S(2)}) copy-start(f32[1076]{0:T(1024)} %param.31) | copy-start | bytes 12916
  72.3 51.8 %all-gather.11.cloned.1.call-start = ((), (), s32[]{:S(2)}) async-start(), calls=%async_computation.13 | async-start | bytes 2985984 | tf_op jit(solution)/shard_map/all_gather | solution.py:142
  72.8 79.0 %all-gather.9.cloned.1.call-start = ((), (), s32[]{:S(2)}) async-start(), calls=%async_computation.12 | async-start | bytes 1474560 | tf_op jit(solution)/shard_map/all_gather | solution.py:170
  122.5 60.3 %all-gather.15.cloned.1.call-start = ((), (), s32[]{:S(2)}) async-start(), calls=%async_computation.16 | async-start | bytes 1474560 | tf_op jit(solution)/shard_map/all_gather | solution.py:182
  123.1 91.9 %all-gather.13.cloned.1.call-start = ((), (), s32[]{:S(2)}) async-start(), calls=%async_computation.14 | async-start | bytes 2985984 | tf_op jit(solution)/shard_map/all_gather | solution.py:143
  123.8 148.9 %reduce-scatter.21.cloned.1.call-start = ((), (), s32[]{:S(2)}) async-start(), calls=%async_computation.17 | async-start | bytes 2949120 | tf_op jit(solution)/shard_map/reduce_scatter | solution.py:188
  215.0 6.8 %copy-start.23 = (bf16[1152,1076]{1,0:T(8,128)(2,1)S(1)}, bf16[1152,1076]{1,0:T(8,128)(2,1)}, u32[]{:S(2)}) copy-start(bf16[1152,1076]{1,0:T(8,128)(2,1)} %all-gather.11.cloned.1.call-done) | copy-start | bytes 7437316
  220.8 1.0 copy-start.27
  225.1 78.5 %reduce-scatter.19.cloned.1.call-start = ((), (), s32[]{:S(2)}) async-start(), calls=%async_computation.15 | async-start | bytes 1474560 | tf_op jit(solution)/shard_map/reduce_scatter | solution.py:174
  231.0 72.7 %copy-start.9 = (bf16[128,1152]{1,0:T(8,128)(2,1)S(1)}, bf16[128,1152]{1,0:T(8,128)(2,1)}, u32[]{:S(2)}) copy-start(bf16[128,1152]{1,0:T(8,128)(2,1)} %param.18) | copy-start | bytes 884740
  231.0 72.7 %copy-start.22 = (f32[1152]{0:T(1024)S(1)}, f32[1152]{0:T(1024)}, u32[]{:S(2)}) copy-start(f32[1152]{0:T(1024)} %param.33) | copy-start | bytes 13828
  231.0 103.7 %all-gather.17.cloned.1.call-start = ((), (), s32[]{:S(2)}) async-start(), calls=%async_computation.18 | async-start | bytes 1474560 | tf_op jit(solution)/shard_map/all_gather | solution.py:196
  306.1 68.9 %reduce-scatter.23.cloned.1.call-start = ((), (), s32[]{:S(2)}) async-start(), calls=%async_computation.19 | async-start | bytes 1474560 | tf_op jit(solution)/shard_map/reduce_scatter | solution.py:210
  336.8 1.0 copy-start.11
  338.5 1.0 copy-start.7
  338.5 1.4 copy-start.6
  340.6 1.2 copy-start.12
  340.6 1.4 copy-start.13
  340.6 1.7 copy-start.14
  342.3 3.3 copy-start.25
  345.5 89.4 %reduce-scatter.29.cloned.1.call-start = ((), (), s32[]{:S(2)}) async-start(), calls=%async_computation.22 | async-start | bytes 5971968 | tf_op jit(solution)/shard_map/reduce_scatter | solution.py:262
  351.3 1.3 copy-start.24
  351.4 144.8 %reduce-scatter.27.cloned.1.call-start = ((), (), s32[]{:S(2)}) async-start(), calls=%async_computation.21 | async-start | bytes 5971968 | tf_op jit(solution)/shard_map/reduce_scatter | solution.py:261
  358.0 1.3 copy-start.2
  358.0 1.3 copy-start.4
  358.0 181.5 %reduce-scatter.25.cloned.1.call-start = ((), (), s32[]{:S(2)}) async-start(), calls=%async_computation.20 | async-start | bytes 1990656 | tf_op jit(solution)/shard_map/reduce_scatter | solution.py:260
  361.4 221.5 %reduce-scatter.35.cloned.1.call-start = ((), (), s32[]{:S(2)}) async-start(), calls=%async_computation.25 | async-start | bytes 1990656
  369.2 256.9 %reduce-scatter.33.cloned.1.call-start = ((), (), s32[]{:S(2)}) async-start(), calls=%async_computation.24 | async-start | bytes 1990656
  372.4 297.2 %reduce-scatter.31.cloned.1.call-start = ((), (), s32[]{:S(2)}) async-start(), calls=%async_computation.23 | async-start | bytes 1990656
  374.2 0.9 copy-start.19
  374.2 45.6 %copy-start.8 = (f32[128,1152]{1,0:T(8,128)S(1)}, f32[128,1152]{1,0:T(8,128)}, u32[]{:S(2)}) copy-start(f32[128,1152]{1,0:T(8,128)} %get-tuple-element.107) | copy-start | bytes 1769476
Sparse Core Ops, SparseCore 0:
  12.6 31.9 all-gather.6
  72.4 47.6 reduce-scatter.16
  225.2 47.4 reduce-scatter.20
  274.9 28.6 reduce-scatter.18
  345.6 28.8 reduce-scatter.22
  378.3 56.5 reduce-scatter.28
  439.2 56.8 reduce-scatter.26
  500.1 39.3 reduce-scatter.24
  543.4 39.3 reduce-scatter.34
  586.7 39.4 reduce-scatter.32
  630.1 39.3 reduce-scatter.30
Sparse Core Ops, SparseCore 1:
  74.6 30.3 all-gather.10
  122.6 29.3 all-gather.8
  153.3 29.4 all-gather.14
  184.7 30.3 all-gather.12
  306.2 28.5 all-gather.16
where the time goes:
time: 678 us; the launch traced here: 677 us
  waiting for transfers between devices  482 us (71%)
  blocking collectives  88.1 us (13%)
  matrix products  52 us (8%)
  local copies, waits for them, and re-layouts  21.5 us (3%)
  between operations  16.1 us (2%)
  other arithmetic  15.7 us (2%)
    unnamed x19, waiting for transfers between devices  132 us
    reduce_scatter x1, waiting for transfers between devices, on_device(): lax.psum_scatter(up_grad, 'fsdp', scatter_dimension=0, tiled=True)  61.3 us
    reduce_scatter x1, waiting for transfers between devices, on_device(): lax.psum_scatter(dot_plain(head_out, full_outp), 'tensor', scatter_dimens...  47.2 us
    reduce_scatter x1, waiting for transfers between devices, on_device(): lax.psum_scatter(outp_grad, 'fsdp', scatter_dimension=1, tiled=True)  43.4 us
    reduce_scatter x1, waiting for transfers between devices, on_device(): lax.psum_scatter(dot_right_t(upper_low, full_up), 'tensor', scatter_dimen...  41.7 us
    psum x1, blocking collectives, on_device(): lax.psum((small_terms, head_terms), ('fsdp', 'tensor'))  41.4 us
    all_gather x1, waiting for transfers between devices, on_device(): lax.all_gather(down_weight, 'fsdp', axis=1, tiled=True)  32.2 us
    reduce_scatter x1, waiting for transfers between devices, on_device(): lax.psum_scatter(dot_plain(hidden_low, full_down).astype(jnp.bfloat16), '...  29.5 us
  transfers between devices with their start and end apart: 16, of which 13 were waited for; matrix products, arithmetic and copies ran while one was open for 7% of the time, Pallas kernels for 0%

commit v1 on v0

--- a/solution.py
+++ b/solution.py
@@ -3,6 +3,8 @@
 import jax
 import jax.numpy as jnp
 from jax import lax
+from jax.experimental import pallas as pl
+from jax.experimental.pallas import tpu as pltpu
 from jax.sharding import PartitionSpec as P
 
 D = 1152
@@ -282,9 +284,800 @@
     )
 
 
+MESH_IDS = pl.DeviceIdType.MESH
+LANES = 128
+
+
+def round_up(value, step):
+    return -(-value // step) * step
+
+
+def layer_kernel(
+    shapes,
+    tokens_ref,
+    cotangent_ref,
+    vectors_ref,
+    attn_piece,
+    up_piece,
+    down_piece,
+    layer_ref,
+    input_grad_ref,
+    attn_grad_ref,
+    up_grad_ref,
+    down_grad_ref,
+    vector_grad_ref,
+    attn_w,
+    up_w,
+    down_w,
+    attn_g,
+    up_g,
+    down_g,
+    land_o,
+    land_q,
+    land_u,
+    land_d,
+    first_all,
+    second_all,
+    dy_all,
+    mid_all,
+    head_rows,
+    head_grads,
+    probs_all,
+    mixed_heads,
+    mixed_all,
+    hidden_all,
+    slope_all,
+    upper_all,
+    qkv_grads,
+    part_a,
+    part_b,
+    core_send,
+    core_land,
+    deep_send,
+    deep_land,
+    first_hat,
+    second_hat,
+    mid_rows,
+    mid_grad,
+    row_scale,
+    vec_send,
+    vec_land,
+    far_vectors,
+    send_sems,
+    recv_sems,
+):
+    rows, heads, width, qkv_lanes, piece = shapes
+    bf16, f32 = jnp.bfloat16, jnp.float32
+    pair = 2 * rows
+    out_base = 3 * width
+    win = out_base // LANES * LANES
+    win_shift = out_base - win
+    all_lanes = attn_w.shape[1]
+
+    f = lax.axis_index("fsdp")
+    t = lax.axis_index("tensor")
+    c, k = lax.rem(f, 2), lax.div(f, 2)
+    kx, ky = lax.rem(k, 2), lax.div(k, 2)
+    zl, zh = lax.rem(t, 2), lax.div(t, 2)
+    oc = 1 - c
+    k_x, k_y, k_d = ky * 2 + (1 - kx), (1 - ky) * 2 + kx, (1 - ky) * 2 + (1 - kx)
+    home = c == zh
+    far_t = (1 - zh) * 2 + zl
+    dev_x = {"fsdp": 2 * k_x + c, "tensor": t}
+    dev_y = {"fsdp": 2 * k_y + c, "tensor": t}
+    dev_c = {"fsdp": 2 * k + oc, "tensor": t}
+    dev_z = {"fsdp": f, "tensor": zh * 2 + (1 - zl)}
+    dev_far = {"fsdp": f, "tensor": far_t}
+    dev_far_other = {"fsdp": 2 * k + oc, "tensor": far_t}
+
+    counter = [0]
+    pending = []
+
+    def new_sem():
+        counter[0] += 1
+        return counter[0] - 1
+
+    def remote(src, dst, device, sem, when=None):
+        copy = pltpu.make_async_remote_copy(
+            src_ref=src,
+            dst_ref=dst,
+            send_sem=send_sems.at[sem],
+            recv_sem=recv_sems.at[sem],
+            device_id=device,
+            device_id_type=MESH_IDS,
+        )
+        if when is None:
+            copy.start()
+        else:
+            pl.when(when)(copy.start)
+        pending.append((copy, when))
+
+    def remote_to(src, dst, device, send, recv, when=None):
+        copy = pltpu.make_async_remote_copy(
+            src_ref=src,
+            dst_ref=dst,
+            send_sem=send_sems.at[send],
+            recv_sem=recv_sems.at[recv],
+            device_id=device,
+            device_id_type=MESH_IDS,
+        )
+        if when is None:
+            copy.start()
+        else:
+            pl.when(when)(copy.start)
+        pending.append((copy, when))
+
+    def arrived(dst, sem):
+        pltpu.make_async_copy(dst, dst, recv_sems.at[sem]).wait()
+
+    def block(buf, index, lo, hi):
+        return buf.at[pl.ds(pl.multiple_of(index * piece, piece), piece), lo:hi]
+
+    def aligned(start, size):
+        return pl.ds(pl.multiple_of(start, LANES), size)
+
+    near, deep = zl * pair, (1 - zl) * pair
+
+    def slot(side, core):
+        return aligned(side + core * rows, rows)
+
+    barrier = pltpu.get_barrier_semaphore()
+    peers = (dev_x, dev_y, dev_c, dev_z, dev_far, dev_far_other)
+    for peer in peers:
+        pl.semaphore_signal(barrier, inc=1, device_id=peer, device_id_type=MESH_IDS)
+
+    def spread_start(src, buf, lo, hi):
+        base = counter[0]
+        for _ in range(2):
+            new_sem()
+        take = pl.ds(0, piece)
+        source = src.at[take, lo:hi]
+        target = block(buf, f, lo, hi)
+
+        @pl.when(home)
+        def _():
+            pltpu.make_async_copy(source, target, recv_sems.at[base + c]).start()
+
+        remote_to(
+            source,
+            target,
+            {"fsdp": 2 * k + zh, "tensor": t},
+            base,
+            base + c,
+            when=jnp.logical_not(home),
+        )
+        remote_to(
+            source, target, {"fsdp": 2 * k + zh, "tensor": far_t}, base + 1, base + c
+        )
+        return base
+
+    def gather_start(buf, lo, hi, base):
+        sems = [new_sem() for _ in range(6)]
+        a_own, b_own = block(buf, 2 * k, lo, hi), block(buf, 2 * k + 1, lo, hi)
+        arrived(a_own, base)
+        remote(a_own, a_own, dev_x, sems[0])
+        arrived(b_own, base + 1)
+        remote(b_own, b_own, dev_y, sems[1])
+        remote(a_own, a_own, dev_y, sems[2])
+        remote(b_own, b_own, dev_x, sems[3])
+        return sems
+
+    def gather_forward(buf, lo, hi, sems):
+        a_x, b_y = block(buf, 2 * k_x, lo, hi), block(buf, 2 * k_y + 1, lo, hi)
+        arrived(a_x, sems[0])
+        remote(a_x, a_x, dev_y, sems[4])
+        arrived(b_y, sems[1])
+        remote(b_y, b_y, dev_x, sems[5])
+
+    def gather_finish(buf, lo, hi, sems):
+        arrived(block(buf, 2 * k_y, lo, hi), sems[2])
+        arrived(block(buf, 2 * k_x + 1, lo, hi), sems[3])
+        arrived(block(buf, 2 * k_d, lo, hi), sems[4])
+        arrived(block(buf, 2 * k_d + 1, lo, hi), sems[5])
+
+    def share_start(buf):
+        sems = [new_sem() for _ in range(3)]
+        own = buf.at[slot(near, c)]
+        remote(own, own, dev_z, sems[0])
+        remote(own, own, dev_c, sems[1])
+        return sems
+
+    def share_near(buf, sems):
+        arrived(buf.at[slot(near, oc)], sems[1])
+
+    def share_forward(buf, sems):
+        got = buf.at[slot(deep, c)]
+        arrived(got, sems[0])
+        remote(got, got, dev_c, sems[2])
+
+    def share_deep(buf, sems):
+        arrived(buf.at[slot(deep, oc)], sems[2])
+
+    def sum_deep(which, part):
+        sems = [new_sem() for _ in range(3)]
+        core_send[which, 0] = part[slot(deep, oc), :].astype(bf16)
+        remote(core_send.at[which, 0], core_land.at[which, 0], dev_c, sems[0])
+        return sems
+
+    def sum_pass(which, part, sems):
+        arrived(core_land.at[which, 0], sems[0])
+        total = part[slot(deep, c), :] + core_land[which, 0].astype(f32)
+        deep_send[which] = total.astype(bf16)
+        remote(deep_send.at[which], deep_land.at[which], dev_z, sems[1])
+
+    def sum_near(which, part, sems):
+        core_send[which, 1] = part[slot(near, oc), :].astype(bf16)
+        remote(core_send.at[which, 1], core_land.at[which, 1], dev_c, sems[2])
+
+    def sum_finish(which, part, sems):
+        arrived(core_land.at[which, 1], sems[2])
+        arrived(deep_land.at[which], sems[1])
+        return (
+            part[slot(near, c), :]
+            + core_land[which, 1].astype(f32)
+            + deep_land[which].astype(f32)
+        )
+
+    def reduce_first(grad, land, lo, hi):
+        sems = [new_sem() for _ in range(8)]
+        remote(block(grad, 2 * k_d, lo, hi), land.at[1], dev_y, sems[1])
+        remote(block(grad, 2 * k_d + 1, lo, hi), land.at[3], dev_x, sems[3])
+        remote(block(grad, 2 * k_y, lo, hi), land.at[0], dev_y, sems[0])
+        remote(block(grad, 2 * k_x + 1, lo, hi), land.at[2], dev_x, sems[2])
+        return sems
+
+    def add_into(grad, index, lo, hi, land, place, sem):
+        arrived(land.at[place], sem)
+        at = pl.ds(pl.multiple_of(index * piece, piece), piece)
+        grad[at, lo:hi] = (
+            grad[at, lo:hi].astype(f32) + land[place].astype(f32)
+        ).astype(bf16)
+
+    def reduce_second(grad, land, lo, hi, sems):
+        add_into(grad, 2 * k_x, lo, hi, land, 1, sems[1])
+        remote(block(grad, 2 * k_x, lo, hi), land.at[4], dev_x, sems[4])
+        add_into(grad, 2 * k_y + 1, lo, hi, land, 3, sems[3])
+        remote(block(grad, 2 * k_y + 1, lo, hi), land.at[5], dev_y, sems[5])
+        add_into(grad, 2 * k, lo, hi, land, 0, sems[0])
+        add_into(grad, 2 * k + 1, lo, hi, land, 2, sems[2])
+
+    def reduce_third(grad, land, lo, hi, sems):
+        add_into(grad, 2 * k, lo, hi, land, 4, sems[4])
+        add_into(grad, 2 * k + 1, lo, hi, land, 5, sems[5])
+        extra = (new_sem(), new_sem())
+        away = jnp.logical_not(home)
+        for core in range(2):
+            source = block(grad, 2 * k + core, lo, hi)
+            mine = jnp.logical_and(home, c == core)
+
+            @pl.when(mine)
+            def _():
+                pltpu.make_async_copy(
+                    source, land.at[6], recv_sems.at[sems[6]]
+                ).start()
+
+            remote_to(
+                source,
+                land.at[6],
+                {"fsdp": 2 * k + core, "tensor": t},
+                extra[0],
+                sems[6],
+                when=jnp.logical_and(home, c != core),
+            )
+            remote_to(
+                source,
+                land.at[7],
+                {"fsdp": 2 * k + core, "tensor": far_t},
+                sems[6 + core],
+                sems[7],
+                when=away,
+            )
+
+    def reduce_finish(land, sems):
+        arrived(land.at[6], sems[6])
+        arrived(land.at[7], sems[7])
+        return land[6].astype(f32) + land[7].astype(f32)
+
+    first_gain, first_shift = vectors_ref[0:1, :], vectors_ref[1:2, :]
+    out_bias, second_gain = vectors_ref[2:3, :], vectors_ref[3:4, :]
+    second_shift, down_bias = vectors_ref[4:5, :], vectors_ref[5:6, :]
+
+    with jax.named_scope("norm_one"):
+        token_rows = tokens_ref[...].astype(f32)
+        normed, hat, inv_scale = norm_rows(token_rows, first_gain, first_shift)
+        first_all[slot(near, c), :] = normed.astype(bf16)
+        first_hat[...] = hat
+        row_scale[0] = jnp.broadcast_to(inv_scale, row_scale.shape[1:])
+        dy_all[slot(near, c), :] = cotangent_ref[...]
+        vec_send[0, 5:6, :] = jnp.sum(cotangent_ref[...].astype(f32), axis=0, keepdims=True)
+
+    with jax.named_scope("entry"):
+        pl.semaphore_wait(barrier, len(peers))
+
+    vec_sem = new_sem()
+    remote(vectors_ref, far_vectors, dev_far, vec_sem)
+    q_base = spread_start(attn_piece, attn_w, 0, qkv_lanes)
+    first_sems = share_start(first_all)
+    o_base = spread_start(attn_piece, attn_w, qkv_lanes, all_lanes)
+    u_base = spread_start(up_piece, up_w, 0, up_w.shape[1])
+    dy_sems = share_start(dy_all)
+    d_base = spread_start(down_piece, down_w, 0, down_w.shape[1])
+
+    with jax.named_scope("clear"):
+        head_rows[...] = jnp.zeros_like(head_rows)
+        head_grads[...] = jnp.zeros_like(head_grads)
+        mixed_all[...] = jnp.zeros_like(mixed_all)
+        qkv_grads[...] = jnp.zeros_like(qkv_grads)
+
+    with jax.named_scope("weights_q"):
+        q_sems = gather_start(attn_w, 0, qkv_lanes, q_base)
+    with jax.named_scope("share_first"):
+        share_forward(first_all, first_sems)
+    with jax.named_scope("weights_q2"):
+        gather_forward(attn_w, 0, qkv_lanes, q_sems)
+        o_sems = gather_start(attn_w, qkv_lanes, all_lanes, o_base)
+        arrived(far_vectors, vec_sem)
+        share_near(first_all, first_sems)
+        share_deep(first_all, first_sems)
+    with jax.named_scope("weights_q3"):
+        gather_finish(attn_w, 0, qkv_lanes, q_sems)
+
+    def unit_vector(row):
+        return jnp.where(home, vectors_ref[row : row + 1, :], far_vectors[row : row + 1, :])
+
+    qkv_bias = unit_vector(6)[:, :qkv_lanes]
+    for side_at in range(2):
+        with jax.named_scope("qkv"):
+            side_rows = slice(side_at * pair, (side_at + 1) * pair)
+            done = dot_plain(first_all[side_rows, :], attn_w[:, :qkv_lanes])
+            done = (done + qkv_bias).astype(bf16)
+            for image in range(2):
+                to = slice(image * pair + side_at * rows, image * pair + (side_at + 1) * rows)
+                for head in range(3 * heads):
+                    head_rows[head, to, :HD] = done[
+                        image * rows : (image + 1) * rows, head * HD : (head + 1) * HD
+                    ]
+    with jax.named_scope("weights_u"):
+        gather_forward(attn_w, qkv_lanes, all_lanes, o_sems)
+        u_sems = gather_start(up_w, 0, up_w.shape[1], u_base)
+        share_forward(dy_all, dy_sems)
+
+    scale = HD ** (-0.5)
+
+    def image_head(step):
+        head, image = lax.rem(step, heads), lax.div(step, heads)
+        return head, aligned(image * pair, pair)
+
+    def attend(step, carry):
+        head, span = image_head(step)
+        queries, keys_part = head_rows[head, span, :], head_rows[heads + head, span, :]
+        values = head_rows[2 * heads + head, span, :]
+        scores = dot_right_t(queries, keys_part) * scale
+        expo = jnp.exp(scores - jnp.max(scores, axis=1, keepdims=True))
+        probs = expo / jnp.sum(expo, axis=1, keepdims=True)
+        probs_all[step] = probs
+        mixed_heads[head, span, :] = dot_plain(probs.astype(bf16), values).astype(bf16)
+        return carry
+
+    with jax.named_scope("attend"):
+        lax.fori_loop(0, 2 * heads, attend, 0)
+
+    def pack(target, source, count, base):
+        for side_at in range(2):
+            for image in range(2):
+                at = slice(side_at * pair + image * rows, side_at * pair + (image + 1) * rows)
+                take = slice(image * pair + side_at * rows, image * pair + (side_at + 1) * rows)
+                for head in range(count):
+                    lo = base + head * HD
+                    target[at, lo : lo + HD] = source[head, take, :HD]
+
+    with jax.named_scope("mix"):
+        pack(mixed_all, mixed_heads, heads, win_shift)
+
+    def half(side):
+        return aligned(side, pair)
+
+    with jax.named_scope("weights_o"):
+        gather_finish(attn_w, qkv_lanes, all_lanes, o_sems)
+    with jax.named_scope("out"):
+        part_a[half(deep), :] = dot_right_t(mixed_all[half(deep), :], attn_w[:, win:])
+        out_sems = sum_deep(0, part_a)
+        part_a[half(near), :] = dot_right_t(mixed_all[half(near), :], attn_w[:, win:])
+    with jax.named_scope("out_pass"):
+        sum_pass(0, part_a, out_sems)
+        sum_near(0, part_a, out_sems)
+    with jax.named_scope("weights_u2"):
+        gather_forward(up_w, 0, up_w.shape[1], u_sems)
+        d_sems = gather_start(down_w, 0, down_w.shape[1], d_base)
+    with jax.named_scope("out_finish"):
+        attn_rows = sum_finish(0, part_a, out_sems)
+    with jax.named_scope("norm_two"):
+        middle = tokens_ref[...].astype(f32) + attn_rows + out_bias
+        mid_rows[...] = middle
+        normed, hat, inv_scale = norm_rows(middle, second_gain, second_shift)
+        second_all[slot(near, c), :] = normed.astype(bf16)
+        second_hat[...] = hat
+        row_scale[1] = jnp.broadcast_to(inv_scale, row_scale.shape[1:])
+        second_sems = share_start(second_all)
+    with jax.named_scope("weights_u3"):
+        gather_finish(up_w, 0, up_w.shape[1], u_sems)
+        share_near(second_all, second_sems)
+
+    up_bias = unit_vector(7)
+    chunk = 32
+
+    def raise_half(side):
+        part_b[half(side), :] = dot_plain(second_all[half(side), :], up_w[...])
+
+        def gelu_rows(step, carry):
+            at = pl.ds(pl.multiple_of(side + step * chunk, chunk), chunk)
+            value, slope = gelu_pair(part_b[at, :] + up_bias)
+            hidden_all[at, :] = value.astype(bf16)
+            slope_all[at, :] = slope
+            return carry
+
+        lax.fori_loop(0, pair // chunk, gelu_rows, 0)
+
+    with jax.named_scope("up_near"):
+        raise_half(near)
+    with jax.named_scope("share_second"):
+        share_forward(second_all, second_sems)
+        share_near(dy_all, dy_sems)
+        share_deep(dy_all, dy_sems)
+        share_deep(second_all, second_sems)
+    with jax.named_scope("up_deep"):
+        raise_half(deep)
+
+    tile = 3 * LANES
+
+    def outer(grad, left, right, lo, hi, more=None):
+        def rows_of(step, carry):
+            at = aligned(step * tile, tile)
+            total = dot_left_t(left[:, at], right)
+            if more is not None:
+                total = total + dot_left_t(more[0][:, at], more[1])
+            grad[at, lo:hi] = total.astype(bf16)
+            return carry
+
+        lax.fori_loop(0, D // tile, rows_of, 0)
+
+    with jax.named_scope("weights_d2"):
+        gather_forward(down_w, 0, down_w.shape[1], d_sems)
+    with jax.named_scope("down_grad"):
+        outer(down_g, dy_all, hidden_all[...], 0, down_g.shape[1])
+        down_reduce = reduce_first(down_g, land_d, 0, down_g.shape[1])
+    with jax.named_scope("weights_d3"):
+        gather_finish(down_w, 0, down_w.shape[1], d_sems)
+
+    def lower_half(side):
+        part_b[half(side), :] = dot_plain(dy_all[half(side), :], down_w[...])
+
+        def slope_rows(step, total):
+            at = pl.ds(pl.multiple_of(side + step * chunk, chunk), chunk)
+            low = (part_b[at, :] * slope_all[at, :]).astype(bf16)
+            upper_all[at, :] = low
+            return total + jnp.sum(low.astype(f32), axis=0, keepdims=True)
+
+        return lax.fori_loop(
+            0, pair // chunk, slope_rows, jnp.zeros((1, part_b.shape[1]), f32)
+        )
+
+    with jax.named_scope("lower_deep"):
+        up_bias_sum = lower_half(deep)
+        part_a[half(deep), :] = dot_right_t(upper_all[half(deep), :], up_w[...])
+        second_sum_sems = sum_deep(1, part_a)
+    with jax.named_scope("lower_near"):
+        up_bias_sum = up_bias_sum + lower_half(near)
+        vec_send[0, 6:7, :] = up_bias_sum
+    with jax.named_scope("second_pass"):
+        sum_pass(1, part_a, second_sum_sems)
+    with jax.named_scope("second_near"):
+        part_a[half(near), :] = dot_right_t(upper_all[half(near), :], up_w[...])
+        sum_near(1, part_a, second_sum_sems)
+    with jax.named_scope("up_grad"):
+        outer(up_g, second_all, upper_all[...], 0, up_g.shape[1])
+        up_reduce = reduce_first(up_g, land_u, 0, up_g.shape[1])
+    with jax.named_scope("second_finish"):
+        second_grad = sum_finish(1, part_a, second_sum_sems)
+    with jax.named_scope("norm_two_back"):
+        back, gain_sum, shift_sum = norm_back(
+            second_grad, second_hat[...], row_scale[1][:, :1], second_gain
+        )
+        vec_send[0, 3:4, :] = gain_sum[None, :]
+        vec_send[0, 4:5, :] = shift_sum[None, :]
+        total = cotangent_ref[...].astype(f32) + back
+        mid_grad[...] = total
+        low = total.astype(bf16)
+        mid_all[slot(near, c), :] = low
+        vec_send[0, 2:3, :] = jnp.sum(low.astype(f32), axis=0, keepdims=True)
+        mid_sems = share_start(mid_all)
+    with jax.named_scope("mlp_out"):
+        part_b[half(deep), :] = dot_right_t(hidden_all[half(deep), :], down_w[...])
+        mlp_sems = sum_deep(2, part_b)
+        part_b[half(near), :] = dot_right_t(hidden_all[half(near), :], down_w[...])
+        sum_pass(2, part_b, mlp_sems)
+        sum_near(2, part_b, mlp_sems)
+    with jax.named_scope("down_reduce2"):
+        reduce_second(down_g, land_d, 0, down_g.shape[1], down_reduce)
+
+    def head_half(side_at):
+        side_rows = slice(side_at * pair, (side_at + 1) * pair)
+        done = dot_plain(mid_all[side_rows, :], attn_w[:, win:]).astype(bf16)
+        for image in range(2):
+            to = slice(image * pair + side_at * rows, image * pair + (side_at + 1) * rows)
+            for head in range(heads):
+                lo = win_shift + head * HD
+                head_grads[head, to, :HD] = done[image * rows : (image + 1) * rows, lo : lo + HD]
+
+    with jax.named_scope("share_mid"):
+        share_forward(mid_all, mid_sems)
+        share_near(mid_all, mid_sems)
+        share_deep(mid_all, mid_sems)
+    with jax.named_scope("head_grad"):
+        head_half(0)
+        head_half(1)
+    with jax.named_scope("out_grad"):
+        skip = qkv_lanes - win
+        outer(attn_g, mid_all, mixed_all[:, skip:], qkv_lanes, all_lanes)
+        out_reduce = reduce_first(attn_g, land_o, qkv_lanes, all_lanes)
+
+    def attend_back(step, carry):
+        head, span = image_head(step)
+        queries, keys_part = head_rows[head, span, :], head_rows[heads + head, span, :]
+        values, grads = head_rows[2 * heads + head, span, :], head_grads[head, span, :]
+        probs = probs_all[step]
+        value_grad = dot_left_t(probs.astype(bf16), grads)
+        prob_grad = dot_right_t(grads, values)
+        row_dot = jnp.sum(probs * prob_grad, axis=1, keepdims=True)
+        score_grad = (probs * (prob_grad - row_dot)).astype(bf16)
+        query_grad = dot_plain(score_grad, keys_part) * scale
+        key_grad = dot_left_t(score_grad, queries) * scale
+        head_rows[head, span, :] = query_grad.astype(bf16)
+        head_rows[heads + head, span, :] = key_grad.astype(bf16)
+        head_rows[2 * heads + head, span, :] = value_grad.astype(bf16)
+        return carry
+
+    with jax.named_scope("attend_back"):
+        lax.fori_loop(0, 2 * heads, attend_back, 0)
+    with jax.named_scope("pack_back"):
+        pack(qkv_grads, head_rows, 3 * heads, 0)
+    with jax.named_scope("first_deep"):
+        part_a[half(deep), :] = dot_right_t(
+            qkv_grads[half(deep), :qkv_lanes], attn_w[:, :qkv_lanes]
+        )
+        first_sum_sems = sum_deep(3, part_a)
+        part_a[half(near), :] = dot_right_t(
+            qkv_grads[half(near), :qkv_lanes], attn_w[:, :qkv_lanes]
+        )
+        sum_pass(3, part_a, first_sum_sems)
+        sum_near(3, part_a, first_sum_sems)
+    with jax.named_scope("qkv_grad"):
+        outer(attn_g, first_all, qkv_grads[:, :win], 0, win)
+        outer(
+            attn_g,
+            first_all,
+            qkv_grads[:, win:qkv_lanes],
+            win,
+            qkv_lanes,
+            more=(mid_all, mixed_all[:, :skip]),
+        )
+        qkv_reduce = reduce_first(attn_g, land_q, 0, qkv_lanes)
+        vec_send[0, 7:8, :] = jnp.sum(qkv_grads[...].astype(f32), axis=0, keepdims=True)
+    with jax.named_scope("mlp_finish"):
+        mlp_rows = sum_finish(2, part_b, mlp_sems)
+        layer_ref[...] = (mid_rows[...] + mlp_rows + down_bias).astype(bf16)
+    with jax.named_scope("reduce_tail"):
+        reduce_third(down_g, land_d, 0, down_g.shape[1], down_reduce)
+        reduce_second(up_g, land_u, 0, up_g.shape[1], up_reduce)
+        reduce_second(attn_g, land_o, qkv_lanes, all_lanes, out_reduce)
+    with jax.named_scope("first_finish"):
+        first_grad = sum_finish(3, part_a, first_sum_sems)
+        back, gain_sum, shift_sum = norm_back(
+            first_grad, first_hat[...], row_scale[0][:, :1], first_gain
+        )
+        input_grad_ref[...] = mid_grad[...] + back
+        vec_send[0, 0:1, :] = gain_sum[None, :]
+        vec_send[0, 1:2, :] = shift_sum[None, :]
+
+    def vector_step(step, device):
+        sem = new_sem()
+        remote(vec_send.at[step], vec_land.at[step], device, sem)
+        return sem
+
+    def vector_add(step, sem):
+        arrived(vec_land.at[step], sem)
+        vec_send[step + 1] = vec_send[step] + vec_land[step]
+
+    with jax.named_scope("vec_x"):
+        sem = vector_step(0, dev_x)
+        reduce_second(attn_g, land_q, 0, qkv_lanes, qkv_reduce)
+        vector_add(0, sem)
+    with jax.named_scope("vec_y"):
+        sem = vector_step(1, dev_y)
+        reduce_third(up_g, land_u, 0, up_g.shape[1], up_reduce)
+        reduce_third(attn_g, land_o, qkv_lanes, all_lanes, out_reduce)
+        vector_add(1, sem)
+    with jax.named_scope("vec_far"):
+        sem = vector_step(2, dev_far)
+        down_grad_ref[...] = reduce_finish(land_d, down_reduce)
+        vector_add(2, sem)
+    with jax.named_scope("vec_z"):
+        sem = vector_step(3, dev_z)
+        reduce_third(attn_g, land_q, 0, qkv_lanes, qkv_reduce)
+        arrived(vec_land.at[3], sem)
+        vec_send[4, 0:6, :] = vec_send[3, 0:6, :] + vec_land[3, 0:6, :]
+        vec_send[4, 6:8, :] = vec_send[3, 6:8, :]
+    with jax.named_scope("vec_c"):
+        sem = vector_step(4, dev_c)
+        up_grad_ref[...] = reduce_finish(land_u, up_reduce)
+        attn_grad_ref[:, qkv_lanes:all_lanes] = reduce_finish(land_o, out_reduce)
+        arrived(vec_land.at[4], sem)
+        vector_grad_ref[0:6, :] = vec_send[4, 0:6, :] + vec_land[4, 0:6, :]
+        vector_grad_ref[6:8, :] = jnp.where(home, vec_send[4, 6:8, :], vec_land[4, 6:8, :])
+    with jax.named_scope("last"):
+        attn_grad_ref[:, :qkv_lanes] = reduce_finish(land_q, qkv_reduce)
+
+    with jax.named_scope("drain"):
+        for copy, when in pending:
+            if when is None:
+                copy.wait_send()
+            else:
+                pl.when(when)(copy.wait_send)
+
+
+def fused_step(
+    tokens,
+    cotangent,
+    first_gain,
+    first_shift,
+    query_weight,
+    key_weight,
+    value_weight,
+    query_bias,
+    value_bias,
+    out_weight,
+    out_bias,
+    second_gain,
+    second_shift,
+    up_weight,
+    up_bias,
+    down_weight,
+    down_bias,
+):
+    bf16, f32 = jnp.bfloat16, jnp.float32
+    rows, piece, width, units = (
+        tokens.shape[0],
+        query_weight.shape[0],
+        query_weight.shape[1],
+        up_weight.shape[1],
+    )
+    heads = width // HD
+    group = 4 * rows
+    qkv_lanes = round_up(3 * width, LANES)
+    attn_lanes = round_up(4 * width, LANES)
+    ff_lanes = round_up(units, LANES)
+    win = 3 * width // LANES * LANES
+
+    def padded(array, lanes):
+        return jnp.pad(array, ((0, 0), (0, lanes - array.shape[1])))
+
+    attn_piece = padded(
+        jnp.concatenate((query_weight, key_weight, value_weight, out_weight.T), axis=1),
+        attn_lanes,
+    )
+    up_piece = padded(up_weight, ff_lanes)
+    down_piece = padded(down_weight.T, ff_lanes)
+    qkv_bias = jnp.concatenate((query_bias, jnp.zeros_like(query_bias), value_bias))
+    vectors = jnp.stack(
+        (
+            first_gain,
+            first_shift,
+            out_bias,
+            second_gain,
+            second_shift,
+            down_bias,
+            jnp.pad(qkv_bias, (0, D - 3 * width)),
+            jnp.pad(up_bias, (0, D - units)),
+        )
+    )
+    vmem = pl.BlockSpec(memory_space=pltpu.VMEM)
+    place = pl.BlockSpec(memory_space=pl.ANY)
+    sem_count = 128
+    o_lanes = attn_lanes - qkv_lanes
+    scratch = [
+        pltpu.VMEM((D, attn_lanes), bf16),
+        pltpu.VMEM((D, ff_lanes), bf16),
+        pltpu.VMEM((D, ff_lanes), bf16),
+        pltpu.VMEM((D, attn_lanes), bf16),
+        pltpu.VMEM((D, ff_lanes), bf16),
+        pltpu.VMEM((D, ff_lanes), bf16),
+        pltpu.VMEM((8, piece, o_lanes), bf16),
+        pltpu.VMEM((8, piece, qkv_lanes), bf16),
+        pltpu.VMEM((8, piece, ff_lanes), bf16),
+        pltpu.VMEM((8, piece, ff_lanes), bf16),
+        pltpu.VMEM((group, D), bf16),
+        pltpu.VMEM((group, D), bf16),
+        pltpu.VMEM((group, D), bf16),
+        pltpu.VMEM((group, D), bf16),
+        pltpu.VMEM((3 * heads, group, LANES), bf16),
+        pltpu.VMEM((heads, group, LANES), bf16),
+        pltpu.VMEM((2 * heads, 2 * rows, 2 * rows), f32),
+        pltpu.VMEM((heads, group, LANES), bf16),
+        pltpu.VMEM((group, attn_lanes - win), bf16),
+        pltpu.VMEM((group, ff_lanes), bf16),
+        pltpu.VMEM((group, ff_lanes), f32),
+        pltpu.VMEM((group, ff_lanes), bf16),
+        pltpu.VMEM((group, attn_lanes), bf16),
+        pltpu.VMEM((group, D), f32),
+        pltpu.VMEM((group, D), f32),
+        pltpu.VMEM((4, 2, rows, D), bf16),
+        pltpu.VMEM((4, 2, rows, D), bf16),
+        pltpu.VMEM((4, rows, D), bf16),
+        pltpu.VMEM((4, rows, D), bf16),
+        pltpu.VMEM((rows, D), f32),
+        pltpu.VMEM((rows, D), f32),
+        pltpu.VMEM((rows, D), f32),
+        pltpu.VMEM((rows, D), f32),
+        pltpu.VMEM((2, rows, LANES), f32),
+        pltpu.VMEM((5, 8, D), f32),
+        pltpu.VMEM((5, 8, D), f32),
+        pltpu.VMEM((8, D), f32),
+        pltpu.SemaphoreType.DMA((sem_count,)),
+        pltpu.SemaphoreType.DMA((sem_count,)),
+    ]
+    shapes = (rows, heads, width, qkv_lanes, piece)
+
+    def body(*refs):
+        layer_kernel(shapes, *refs)
+
+    layer_out, input_grad, attn_grad, up_grad, down_grad, vector_grad = pl.pallas_call(
+        body,
+        out_shape=(
+            jax.ShapeDtypeStruct((rows, D), bf16),
+            jax.ShapeDtypeStruct((rows, D), f32),
+            jax.ShapeDtypeStruct((piece, attn_lanes), f32),
+            jax.ShapeDtypeStruct((piece, ff_lanes), f32),
+            jax.ShapeDtypeStruct((piece, ff_lanes), f32),
+            jax.ShapeDtypeStruct((8, D), f32),
+        ),
+        in_specs=[vmem, vmem, vmem, place, place, place],
+        out_specs=(vmem,) * 6,
+        scratch_shapes=scratch,
+        compiler_params=pltpu.CompilerParams(
+            collective_id=0, has_side_effects=True, vmem_limit_bytes=67043328
+        ),
+        name="layer",
+    )(tokens, cotangent, vectors, attn_piece, up_piece, down_piece)
+    return (
+        layer_out,
+        input_grad,
+        vector_grad[0],
+        vector_grad[1],
+        attn_grad[:, :width],
+        attn_grad[:, width : 2 * width],
+        attn_grad[:, 2 * width : 3 * width],
+        vector_grad[7, :width],
+        vector_grad[7, 2 * width : 3 * width],
+        attn_grad[:, 3 * width : 4 * width].T,
+        vector_grad[2],
+        vector_grad[3],
+        vector_grad[4],
+        up_grad[:, :units],
+        vector_grad[6, :units],
+        down_grad[:, :units].T,
+        vector_grad[5],
+    )
+
+
+def pick_step(mesh):
+    if mesh.shape["fsdp"] == 8 and mesh.shape["tensor"] == 4:
+        return fused_step
+    return on_device
+
+
 def solution(mesh):
     return jax.shard_map(
-        on_device,
+        pick_step(mesh),
         mesh=mesh,
         in_specs=(
             P(("fsdp", "tensor"), None),

time: 678 us -> 199 us (0.29)
  waiting for transfers between devices: 482 us -> 0 us
  Pallas kernels: 0 us -> 178 us
  blocking collectives: 88.1 us -> 0 us
  matrix products: 52 us -> 0 us
  between operations: 16.1 us -> 0.7 us
  other arithmetic: 15.7 us -> 0.77 us
    reduce_scatter x7 -> x0, waiting for transfers between devices: 236 us -> none  [the longest x1 61.3 us: on_device(): lax.psum_scatter(up_grad, 'fsdp', scatter_dimension=0, tiled=True)]
    pallas_call x0 -> x1, Pallas kernels: none -> 178 us  [fused_step(): pl.pallas_call(body, out_shape=(jax.ShapeDtypeStruct((rows, D), bf16), ja...]
    unnamed x19 -> x0, waiting for transfers between devices: 132 us -> none
    all_gather x6 -> x0, waiting for transfers between devices: 114 us -> none  [the longest x1 32.2 us: on_device(): lax.all_gather(down_weight, 'fsdp', axis=1, tiled=True)]
    dot_general x18 -> x0, matrix products: 52 us -> none  [the longest x4 17.9 us: dot_plain(): return jnp.dot(left, right, preferred_element_type=jnp.float32)]
    all_gather x4 -> x0, blocking collectives: 46.7 us -> none  [the longest x1 14 us: on_device(): lax.all_gather(query_weight, 'fsdp', axis=0, tiled=True)]
    psum x1 -> x0, blocking collectives: 41.4 us -> none  [on_device(): lax.psum((small_terms, head_terms), ('fsdp', 'tensor'))]
    unnamed x70 -> x19, local copies, waits for them, and re-layouts: 14.1 us -> 3.67 us
  transfers between devices with their start and end apart: 16 -> 0, of which waited for: 13 -> 0; matrix products, arithmetic and copies ran while one was open for 7% -> 0% of each run, Pallas kernels for 0% -> 0%
where the time goes in v1:
time: 199 us
  Pallas kernels  178 us (89%)
  local copies, waits for them, and re-layouts  19.4 us (10%)
    pallas_call x1, Pallas kernels, fused_step(): pl.pallas_call(body, out_shape=(jax.ShapeDtypeStruct((rows, D), bf16), ja...  178 us
    another operation x9, local copies, waits for them, and re-layouts, fused_step(): jnp.stack((first_gain, first_shift, out_bias, second_gain, second_shift,...  4.92 us

profile of v1, /device:TPU:1, one launch (start us, length us, event | category | flops | bytes accessed | tf_op | source)
XLA Modules:
  0.0 198.7 jit_solution(2393401983030988630)
XLA Ops:
  0.7 0.0 copy-start.6
  0.7 0.7 stack.27
  1.4 0.7 stack.28
  2.1 0.7 stack.29
  2.8 0.7 stack.30
  3.5 0.7 stack.31
  4.2 0.7 stack.32
  4.9 0.8 select_maximum_fusion
  5.7 0.7 pad.16
  6.4 0.7 stack.35.refs_2_
  7.1 0.0 copy-done.6
  7.1 0.0 copy-start.3
  7.1 2.0 %concatenate.7.refs_3_ = bf16[144,1152]{1,0:T(8,128)(2,1)} concatenate(bf16[144,288]{1,0:T(8,128)(2,1)S(1)} %copy-done.6, bf16[144,288]{1,0:T(8,128)(2,1)} %param.22, bf16[144,288]{1,0:T(8,128)(2,1)} %param.23, bf16[144,288]{1,0:T(8,128)(2,1)} %bitcast.9), dimensions={1} | concatenate | bytes 663552 | tf_op jit(solution)/shard_map/concatenate | solution.py:965
  9.1 0.0 copy-done.3
  9.1 0.0 copy-start.4
  9.1 0.8 pad.17.refs_4_
  9.8 0.3 copy-done.4
  10.2 0.8 pad.18.refs_5_
  10.9 177.8 %layer.1 = (bf16[128,1152]{1,0:T(8,128)(2,1)}, f32[128,1152]{1,0:T(8,128)}, f32[144,1152]{1,0:T(8,128)}, f32[144,1152]{1,0:T(8,128)}, f32[144,1152]{1,0:T(8,128)}, /*index=5*/f32[8,1152]{1,0:T(8,128)}) custom-call(bf16[128,1152]{1,0:T(8,128)(2,1)} %refs_0_.1, bf16[128,1152]{1,0:T(8,128)(2,1)} %refs_1_.1, f32[8,1152]{1,0:T(8,128)} %stack.35.refs_2_, ...), custom_call_target="tpu_custom_call" | custom-call | tf_op jit(solution)/shard_map/layer/pallas_call | solution.py:1033
  188.7 0.0 copy-start.7
  188.8 1.4 slice_reduce_fusion.7
  190.2 1.4 slice_reduce_fusion.1
  191.6 0.0 copy-done.7
  191.6 0.7 slice_reduce_fusion
  192.3 0.0 copy-start
  192.3 2.0 %slice_bitcast_fusion = f32[1076,144]{0,1:T(8,128)} fusion(f32[144,1152]{1,0:T(8,128)} %get-tuple-element.28), kind=kLoop, calls=%fused_computation | loop fusion | bytes 1239552 | tf_op jit(solution)/shard_map/transpose | solution.py:1067
  194.3 0.0 copy-done
  194.3 0.0 copy-start.5
  194.3 1.1 slice_bitcast_fusion.1
  195.4 0.0 copy-start.2
  195.4 0.0 copy-done.5
  195.4 0.7 copy.37
  196.1 0.5 copy-done.2
  196.6 0.0 copy-start.1
  196.6 0.8 copy.38
  197.4 0.5 copy-done.1
  197.9 0.8 copy.39
  (3 shorter events, 0.0 us)
Async XLA Ops:
  0.7 6.4 %copy-start.6 = (bf16[144,288]{1,0:T(8,128)(2,1)S(1)}, bf16[144,288]{1,0:T(8,128)(2,1)}, u32[]{:S(2)}) copy-start(bf16[144,288]{1,0:T(8,128)(2,1)} %param.21) | copy-start | bytes 248836
  7.1 2.0 %copy-start.3 = (bf16[144,1076]{1,0:T(8,128)(2,1)S(1)}, bf16[144,1076]{1,0:T(8,128)(2,1)}, u32[]{:S(2)}) copy-start(bf16[144,1076]{1,0:T(8,128)(2,1)} %param.30) | copy-start | bytes 929668
  9.1 1.1 copy-start.4
  188.7 2.8 %copy-start.7 = (f32[8,1152]{1,0:T(8,128)S(1)}, f32[8,1152]{1,0:T(8,128)}, u32[]{:S(2)}) copy-start(f32[8,1152]{1,0:T(8,128)} %get-tuple-element.25) | copy-start | bytes 110596
  192.3 2.0 %copy-start = (f32[144,1152]{1,0:T(8,128)S(1)}, f32[144,1152]{1,0:T(8,128)}, u32[]{:S(2)}) copy-start(f32[144,1152]{1,0:T(8,128)} %get-tuple-element.26) | copy-start | bytes 1990660
  194.3 1.1 copy-start.5
  195.4 1.2 copy-start.2
  196.6 1.3 copy-start.1

commit v2 on v0

--- a/solution.py
+++ b/solution.py
@@ -1,8 +1,11 @@
 import math
+from types import SimpleNamespace
 
 import jax
 import jax.numpy as jnp
 from jax import lax
+from jax.experimental import pallas as pl
+from jax.experimental.pallas import tpu as pltpu
 from jax.sharding import PartitionSpec as P
 
 D = 1152
@@ -282,9 +285,1122 @@
     )
 
 
+MESH_IDS = pl.DeviceIdType.MESH
+LANES = 128
+
+
+def round_up(value, step):
+    return -(-value // step) * step
+
+
+def row_cuts(count, parts):
+    edges = [min(count, round_up(count * at // parts, 16)) for at in range(parts + 1)]
+    return list(zip(edges[:-1], edges[1:]))
+
+
+class Remote:
+    def __init__(self, send_sems, recv_sems):
+        self.send_sems, self.recv_sems = send_sems, recv_sems
+        self.used = 0
+        self.pending = []
+
+    def sem(self):
+        self.used += 1
+        return self.used - 1
+
+    def sems(self, count):
+        return [self.sem() for _ in range(count)]
+
+    def send(self, src, dst, device, sem, recv=None, when=None):
+        copy = pltpu.make_async_remote_copy(
+            src_ref=src,
+            dst_ref=dst,
+            send_sem=self.send_sems.at[sem],
+            recv_sem=self.recv_sems.at[sem if recv is None else recv],
+            device_id=device,
+            device_id_type=MESH_IDS,
+        )
+        if when is None:
+            copy.start()
+        else:
+            pl.when(when)(copy.start)
+        self.pending.append((copy, when))
+
+    def local(self, src, dst, sem, when):
+        copy = pltpu.make_async_copy(src, dst, self.recv_sems.at[sem])
+        pl.when(when)(copy.start)
+
+    def arrived(self, dst, sem):
+        pltpu.make_async_copy(dst, dst, self.recv_sems.at[sem]).wait()
+
+    def drain(self):
+        for copy, when in self.pending:
+            if when is None:
+                copy.wait_send()
+            else:
+                pl.when(when)(copy.wait_send)
+
+
+def layer_kernel(shapes, names, *refs):
+    rows, heads, width, units, qkv_lanes, piece = shapes
+    inputs, outputs, scratch = names
+    hbm = SimpleNamespace(**dict(zip(inputs, refs[: len(inputs)], strict=True)))
+    refs = refs[len(inputs) :]
+    out = SimpleNamespace(**dict(zip(outputs, refs[: len(outputs)], strict=True)))
+    refs = refs[len(outputs) :]
+    held = SimpleNamespace(**dict(zip(inputs, refs[: len(inputs)], strict=True)))
+    refs = refs[len(inputs) :]
+    ref = SimpleNamespace(**dict(zip(scratch, refs, strict=True)))
+    bf16, f32 = jnp.bfloat16, jnp.float32
+    attn_w, up_w, down_w = ref.attn_w, ref.up_w, ref.down_w
+    attn_g, up_g, down_g = ref.attn_g, ref.up_g, ref.down_g
+    first_all, second_all = ref.first_all, ref.second_all
+    dy_all, mid_all = ref.dy_all, ref.mid_all
+    head_rows, head_grads = ref.head_rows, ref.head_grads
+    mixed_all, hidden_all, upper_all = ref.mixed_all, ref.hidden_all, ref.upper_all
+    slope_all, qkv_grads = ref.slope_all, ref.qkv_grads
+    part_a, part_b, vectors = ref.part_a, ref.part_b, ref.vectors
+    pair, fourth = 2 * rows, rows // 2
+    out_base = 3 * width
+    win = out_base // LANES * LANES
+    win_shift = out_base - win
+    skip = qkv_lanes - win
+    all_lanes, ff_lanes = attn_w.shape[1], up_w.shape[1]
+
+    f = lax.axis_index("fsdp")
+    t = lax.axis_index("tensor")
+    c, k = lax.rem(f, 2), lax.div(f, 2)
+    kx, ky = lax.rem(k, 2), lax.div(k, 2)
+    zl, zh = lax.rem(t, 2), lax.div(t, 2)
+    oc, ox = 1 - c, 1 - kx
+    k_x, k_y, k_d = ky * 2 + ox, (1 - ky) * 2 + kx, (1 - ky) * 2 + ox
+    home = c == zh
+    away = jnp.logical_not(home)
+    stay = kx == zh
+    outer = zl == zh
+    inner = jnp.logical_not(outer)
+    move = jnp.logical_not(stay)
+    far_t = (1 - zh) * 2 + zl
+    dev_x = {"fsdp": 2 * k_x + c, "tensor": t}
+    dev_y = {"fsdp": 2 * k_y + c, "tensor": t}
+    dev_c = {"fsdp": 2 * k + oc, "tensor": t}
+    dev_z = {"fsdp": f, "tensor": zh * 2 + (1 - zl)}
+    dev_far = {"fsdp": f, "tensor": far_t}
+    dev_far_other = {"fsdp": 2 * k + oc, "tensor": far_t}
+    net = Remote(ref.send_sems, ref.recv_sems)
+
+    def aligned(start, size):
+        return pl.ds(pl.multiple_of(start, math.gcd(size, LANES)), size)
+
+    def piece_at(index):
+        return pl.ds(pl.multiple_of(index * piece, piece), piece)
+
+    def block(buf, index, lo=0, hi=None):
+        return buf.at[piece_at(index), lo : buf.shape[1] if hi is None else hi]
+
+    near, deep = zl * pair, (1 - zl) * pair
+
+    def slot(side, place):
+        return aligned(side + place * rows, rows)
+
+    def spread_start(src, buf, lo, hi):
+        base, other = net.sems(2)
+        source, target = src.at[:, lo:hi], block(buf, f, lo, hi)
+        net.local(source, target, base + c, home)
+        to = {"fsdp": 2 * k + zh, "tensor": t}
+        net.send(source, target, to, base, recv=base + c, when=away)
+        to = {"fsdp": 2 * k + zh, "tensor": far_t}
+        net.send(source, target, to, other, recv=base + c)
+        return base
+
+    def gather_start(buf, lo, hi, base):
+        sems = net.sems(6)
+        a_own, b_own = block(buf, 2 * k, lo, hi), block(buf, 2 * k + 1, lo, hi)
+        net.arrived(a_own, base)
+        net.send(a_own, a_own, dev_x, sems[0])
+        net.arrived(b_own, base + 1)
+        net.send(b_own, b_own, dev_y, sems[1])
+        net.send(a_own, a_own, dev_y, sems[2])
+        net.send(b_own, b_own, dev_x, sems[3])
+        return sems
+
+    def gather_forward(buf, lo, hi, sems):
+        a_x, b_y = block(buf, 2 * k_x, lo, hi), block(buf, 2 * k_y + 1, lo, hi)
+        net.arrived(a_x, sems[0])
+        net.send(a_x, a_x, dev_y, sems[4])
+        net.arrived(b_y, sems[1])
+        net.send(b_y, b_y, dev_x, sems[5])
+
+    def gather_finish(buf, lo, hi, sems):
+        net.arrived(block(buf, 2 * k_y, lo, hi), sems[2])
+        net.arrived(block(buf, 2 * k_x + 1, lo, hi), sems[3])
+        net.arrived(block(buf, 2 * k_d, lo, hi), sems[4])
+        net.arrived(block(buf, 2 * k_d + 1, lo, hi), sems[5])
+
+    f_x, f_y, f_d = 2 * k_x + c, 2 * k_y + c, 2 * k_d + c
+
+    class WideGather:
+        def __init__(self, src, buf, wait_at, lo, hi):
+            self.buf, self.lo, self.size = buf, lo, hi - lo
+            self.src, self.wait_at = src.at[lo:hi, :], wait_at.at[lo:hi, :]
+            self.sems = net.sems(9)
+
+        def at(self, index):
+            start = pl.multiple_of(index * piece + self.lo, 16)
+            return self.buf.at[pl.ds(start, self.size), :]
+
+        def start(self, when):
+            own, sems = self.at(f), self.sems
+            stay_now, move_now = jnp.logical_and(stay, when), jnp.logical_and(move, when)
+            net.local(self.src, own, sems[8], stay_now)
+            net.send(self.src, own, dev_far, sems[0], when=stay_now)
+            net.send(self.src, self.wait_at, dev_far, sems[0], when=move_now)
+
+        def beside(self):
+            net.send(self.src, self.at(f), dev_x, self.sems[1], when=move)
+
+        def second(self):
+            own, sems = self.at(f), self.sems
+
+            @pl.when(stay)
+            def _():
+                net.arrived(self.wait_at, sems[0])
+
+            @pl.when(move)
+            def _():
+                net.arrived(own, sems[0])
+
+            net.send(self.wait_at, own, dev_x, sems[1], when=stay)
+
+            @pl.when(stay)
+            def _():
+                net.arrived(own, sems[8])
+
+            net.send(own, own, dev_y, sems[2])
+            net.send(own, own, dev_c, sems[4])
+
+        def third(self):
+            got = self.at(f_x)
+            net.arrived(got, self.sems[1])
+            net.send(got, got, dev_y, self.sems[3])
+            net.send(got, got, dev_c, self.sems[5])
+
+        def fourth(self):
+            for index, sem, to in ((f_y, 2, 6), (f_d, 3, 7)):
+                got = self.at(index)
+                net.arrived(got, self.sems[sem])
+                net.send(got, got, dev_c, self.sems[to])
+
+        def finish(self):
+            for index, sem in ((f, 4), (f_x, 5), (f_y, 6), (f_d, 7)):
+                net.arrived(self.at(index + oc - c), self.sems[sem])
+
+    def share_start(buf):
+        sems = net.sems(3)
+        own = buf.at[slot(near, c)]
+        net.send(own, own, dev_z, sems[0])
+        net.send(own, own, dev_c, sems[1])
+        return sems
+
+    def share_near(buf, sems):
+        net.arrived(buf.at[slot(near, oc)], sems[1])
+
+    def share_forward(buf, sems):
+        got = buf.at[slot(deep, c)]
+        net.arrived(got, sems[0])
+        net.send(got, got, dev_c, sems[2])
+
+    def share_deep(buf, sems):
+        net.arrived(buf.at[slot(deep, oc)], sems[2])
+
+    def sum_deep(which, part):
+        sems = net.sems(3)
+        send = ref.core_send.at[which, 0]
+        send[...] = part[slot(deep, oc), :].astype(bf16)
+        net.send(send, ref.core_land.at[which, 0], dev_c, sems[0])
+        return sems
+
+    def sum_pass(which, part, sems):
+        land, send = ref.core_land.at[which, 0], ref.deep_send.at[which]
+        net.arrived(land, sems[0])
+        send[...] = (part[slot(deep, c), :] + land[...].astype(f32)).astype(bf16)
+        net.send(send, ref.deep_land.at[which], dev_z, sems[1])
+
+    def sum_near(which, part, sems):
+        send = ref.core_send.at[which, 1]
+        send[...] = part[slot(near, oc), :].astype(bf16)
+        net.send(send, ref.core_land.at[which, 1], dev_c, sems[2])
+
+    def sum_finish(which, part, sems):
+        beside, across = ref.core_land.at[which, 1], ref.deep_land.at[which]
+        net.arrived(beside, sems[2])
+        total = part[slot(near, c), :] + beside[...].astype(f32)
+        net.arrived(across, sems[1])
+        return total + across[...].astype(f32)
+
+    def quarter(side, place, which):
+        return aligned(side + place * rows + which * fourth, fourth)
+
+    def wide_share_start(buf):
+        sems = net.sems(6)
+        first, second = buf.at[quarter(near, kx, 0)], buf.at[quarter(near, kx, 1)]
+        net.send(first, first, dev_z, sems[0])
+        net.send(second, second, dev_x, sems[1])
+        net.send(second, second, dev_z, sems[2])
+        net.send(first, first, dev_x, sems[3])
+        return sems
+
+    def wide_share_forward(buf, sems):
+        from_z, from_x = buf.at[quarter(deep, kx, 0)], buf.at[quarter(near, ox, 1)]
+        net.arrived(from_z, sems[0])
+        net.send(from_z, from_z, dev_x, sems[4])
+        net.arrived(from_x, sems[1])
+        net.send(from_x, from_x, dev_z, sems[5])
+
+    def wide_share_near(buf, sems):
+        net.arrived(buf.at[quarter(near, ox, 0)], sems[3])
+
+    def wide_share_deep(buf, sems):
+        net.arrived(buf.at[quarter(deep, kx, 1)], sems[2])
+        net.arrived(buf.at[quarter(deep, ox, 0)], sems[4])
+        net.arrived(buf.at[quarter(deep, ox, 1)], sems[5])
+
+    def plain_share_z(buf):
+        sems = net.sems(3)
+        own = buf.at[slot(near, kx)]
+        net.send(own, own, dev_z, sems[0])
+        return sems
+
+    def plain_share_x(buf, sems):
+        own = buf.at[slot(near, kx)]
+        net.send(own, own, dev_x, sems[1])
+
+    def plain_share_forward(buf, sems):
+        got = buf.at[slot(near, ox)]
+        net.arrived(got, sems[1])
+        net.send(got, got, dev_z, sems[2])
+
+    def plain_share_finish(buf, sems):
+        net.arrived(buf.at[slot(deep, kx)], sems[0])
+        net.arrived(buf.at[slot(deep, ox)], sems[2])
+
+    def wide_send(which, number):
+        return ref.wide_send.at[which, number]
+
+    def wide_land(which, number):
+        return ref.wide_land.at[which, number]
+
+    def wide_push(which, number, value, device, sem):
+        wide_send(which, number)[...] = value.astype(bf16)
+        net.send(wide_send(which, number), wide_land(which, number), device, sem)
+
+    def wide_sum_deep(which, part):
+        sems = net.sems(6)
+        wide_push(which, 0, part[quarter(deep, ox, 0), :], dev_x, sems[0])
+        wide_push(which, 1, part[quarter(deep, ox, 1), :], dev_z, sems[1])
+        wide_push(which, 2, part[quarter(deep, kx, 1), :], dev_z, sems[2])
+        return sems
+
+    def wide_sum_near(which, part, sems):
+        wide_push(which, 3, part[quarter(near, ox, 0), :], dev_x, sems[3])
+
+    def wide_sum_pass(which, part, sems):
+        net.arrived(wide_land(which, 0), sems[0])
+        total = part[quarter(deep, kx, 0), :] + wide_land(which, 0)[...].astype(f32)
+        wide_push(which, 4, total, dev_z, sems[4])
+        net.arrived(wide_land(which, 1), sems[1])
+        total = part[quarter(near, ox, 1), :] + wide_land(which, 1)[...].astype(f32)
+        wide_push(which, 5, total, dev_x, sems[5])
+
+    def wide_sum_finish(which, part, sems):
+        halves = []
+        for half_at, (by_z, by_x) in enumerate(((4, 3), (2, 5))):
+            net.arrived(wide_land(which, by_z), sems[by_z])
+            net.arrived(wide_land(which, by_x), sems[by_x])
+            halves.append(
+                part[quarter(near, kx, half_at), :]
+                + wide_land(which, by_z)[...].astype(f32)
+                + wide_land(which, by_x)[...].astype(f32)
+            )
+        return jnp.concatenate(halves, axis=0)
+
+    def add_into(grad, index, lo, hi, land):
+        at = piece_at(index)
+        total = grad[at, lo:hi].astype(f32) + land[...].astype(f32)
+        grad[at, lo:hi] = total.astype(bf16)
+
+    def guarded(when, action):
+        if when is None:
+            action()
+        else:
+            pl.when(when)(action)
+
+    def reduce_route(core, by_y):
+        if core == 0 or by_y:
+            return dev_y, 2 * k_y + core, 2 * k_x + core, dev_x
+        return dev_x, 2 * k_x + core, 2 * k_y + core, dev_y
+
+    def reduce_first(grad, land, lo, hi, sems, by_y=False, when=None):
+        for distant in (True, False):
+            for core in range(2):
+                device, index, _, _ = reduce_route(core, by_y)
+                index, number = (2 * k_d + core, 1 + 2 * core) if distant else (index, 2 * core)
+                source = block(grad, index, lo, hi)
+                net.send(source, land.at[number], device, sems[number], when=when)
+
+    def reduce_second(grad, land, lo, hi, sems, by_y=False, when=None):
+        def collect(index, number):
+            def action():
+                net.arrived(land.at[number], sems[number])
+                add_into(grad, index, lo, hi, land.at[number])
+
+            guarded(when, action)
+
+        for core in range(2):
+            _, _, index, device = reduce_route(core, by_y)
+            collect(index, 1 + 2 * core)
+            source = block(grad, index, lo, hi)
+            net.send(source, land.at[4 + core], device, sems[4 + core], when=when)
+        for core in range(2):
+            collect(2 * k + core, 2 * core)
+
+    def reduce_third(grad, land, lo, hi, sems):
+        for core in range(2):
+            net.arrived(land.at[4 + core], sems[4 + core])
+            add_into(grad, 2 * k + core, lo, hi, land.at[4 + core])
+            source = block(grad, 2 * k + core, lo, hi)
+            mine, other = jnp.logical_and(home, c == core), jnp.logical_and(home, c != core)
+            net.local(source, land.at[6], sems[6], mine)
+            to = {"fsdp": 2 * k + core, "tensor": t}
+            net.send(source, land.at[6], to, sems[8], recv=sems[6], when=other)
+            to = {"fsdp": 2 * k + core, "tensor": far_t}
+            net.send(source, land.at[7], to, sems[6 + core], recv=sems[7], when=away)
+
+    def reduce_finish(land, sems):
+        net.arrived(land.at[6], sems[6])
+        net.arrived(land.at[7], sems[7])
+        return land[6].astype(f32) + land[7].astype(f32)
+
+    def wide_reduce_first(grad, land):
+        sems = net.sems(8)
+        for number, index in enumerate((f_y, f_d, f, f_x)):
+            net.send(block(grad, index + oc - c), land.at[number], dev_c, sems[number])
+        return sems
+
+    def wide_reduce_second(grad, land, sems):
+        for number, index in enumerate((f_y, f_d)):
+            net.arrived(land.at[number], sems[number])
+            add_into(grad, index, 0, ff_lanes, land.at[number])
+            net.send(block(grad, index), land.at[4 + number], dev_y, sems[4 + number])
+        for number, index in ((2, f), (3, f_x)):
+            net.arrived(land.at[number], sems[number])
+            add_into(grad, index, 0, ff_lanes, land.at[number])
+
+    def wide_reduce_third(grad, land, sems):
+        net.arrived(land.at[5], sems[5])
+        add_into(grad, f_x, 0, ff_lanes, land.at[5])
+        net.send(block(grad, f_x), land.at[6], dev_x, sems[6])
+        net.arrived(land.at[4], sems[4])
+        add_into(grad, f, 0, ff_lanes, land.at[4])
+
+    def wide_reduce_cross(grad, land, sems):
+        net.send(block(grad, f), land.at[7], dev_far, sems[7], when=move)
+
+    def wide_reduce_fourth(grad, land, sems):
+        net.arrived(land.at[6], sems[6])
+        net.send(land.at[6], land.at[7], dev_far, sems[7], when=stay)
+
+    def wide_reduce_finish(grad, land, sems):
+        kept = jnp.where(stay, grad[piece_at(f), :].astype(f32), land[6].astype(f32))
+        net.arrived(land.at[7], sems[7])
+        return kept + land[7].astype(f32)
+
+    vec_own, by_plane, by_chip = ref.vec_own, ref.by_plane, ref.by_chip
+    plane_peers = [lax.rem(t + step, 4) for step in range(1, 4)]
+    chip_peers = [lax.rem(k + step, 4) for step in range(1, 4)]
+
+    def vector_planes():
+        by_plane[t] = vec_own[...]
+        sems = net.sems(3)
+        for sem, plane in zip(sems, plane_peers, strict=True):
+            net.send(vec_own, by_plane.at[t], {"fsdp": f, "tensor": plane}, sem)
+        return sems
+
+    def vector_chips(sems):
+        for sem, step in zip(sems, range(3, 0, -1), strict=True):
+            net.arrived(by_plane.at[lax.rem(t + step, 4)], sem)
+        both = ref.vec_chip
+        total = by_plane[0] + by_plane[1] + by_plane[2] + by_plane[3]
+        shard = by_plane[zl] + by_plane[2 + zl]
+        both[0:6, :] = total[0:6, :]
+        both[6:8, :] = shard[6:8, :]
+        by_chip[k] = both[...]
+        sems = net.sems(3)
+        for sem, chip in zip(sems, chip_peers, strict=True):
+            net.send(both, by_chip.at[k], {"fsdp": 2 * chip + c, "tensor": t}, sem)
+        return sems
+
+    def vector_core(sems):
+        for sem, step in zip(sems, range(3, 0, -1), strict=True):
+            net.arrived(by_chip.at[lax.rem(k + step, 4)], sem)
+        held = ref.vec_core
+        total = by_chip[0] + by_chip[1] + by_chip[2] + by_chip[3]
+        units_total = by_chip[zh] + by_chip[2 + zh]
+        held[0:6, :] = total[0:6, :]
+        held[6:7, :] = units_total[6:7, :]
+        held[7:8, :] = total[7:8, :]
+        sem = net.sem()
+        net.send(held, ref.vec_core_land, dev_c, sem)
+        return sem
+
+    def vector_finish(sem):
+        held, land, done = ref.vec_core, ref.vec_core_land, ref.vec_done
+        net.arrived(land, sem)
+        done[0:7, :] = held[0:7, :] + land[0:7, :]
+        done[7:8, :] = jnp.where(home, held[7:8, :], land[7:8, :])
+
+    barrier = pltpu.get_barrier_semaphore()
+    dev_d = {"fsdp": 2 * k_d + c, "tensor": t}
+    dev_last = {"fsdp": f, "tensor": (1 - zh) * 2 + (1 - zl)}
+    peers = (dev_x, dev_y, dev_d, dev_c, dev_z, dev_far, dev_last, dev_far_other)
+    for peer in peers:
+        pl.semaphore_signal(barrier, inc=1, device_id=peer, device_id_type=MESH_IDS)
+
+    coming = {}
+    for number, name in enumerate(inputs):
+        copy = pltpu.make_async_copy(
+            getattr(hbm, name), getattr(held, name), ref.load_sems.at[number]
+        )
+        copy.start()
+        coming[name] = copy
+    coming = SimpleNamespace(**coming)
+    stores = []
+
+    def store(source, target):
+        sem = ref.load_sems.at[len(inputs) + len(stores)]
+        copy = pltpu.make_async_copy(source, target, sem)
+        copy.start()
+        stores.append(copy)
+
+    attn_piece = ref.attn_piece
+    if all_lanes > 4 * width:
+        attn_piece[:, 4 * width :] = jnp.zeros((piece, all_lanes - 4 * width), bf16)
+    for number, (copy, raw) in enumerate(
+        (
+            (coming.query_w, held.query_w),
+            (coming.key_w, held.key_w),
+            (coming.value_w, held.value_w),
+            (coming.out_w, held.out_w),
+        )
+    ):
+        copy.wait()
+        attn_piece[:, number * width : (number + 1) * width] = raw[...]
+    vectors[...] = jnp.zeros_like(vectors)
+    for number, (copy, raw) in enumerate(
+        (
+            (coming.first_gain, held.first_gain),
+            (coming.first_shift, held.first_shift),
+            (coming.out_bias, held.out_bias),
+            (coming.second_gain, held.second_gain),
+            (coming.second_shift, held.second_shift),
+            (coming.down_bias, held.down_bias),
+        )
+    ):
+        copy.wait()
+        vectors[number : number + 1, :] = raw[...].reshape(1, D)
+    coming.up_bias.wait()
+    vectors[6:7, :units] = held.up_bias[...].reshape(1, units)
+    coming.query_bias.wait()
+    vectors[7:8, :width] = held.query_bias[...].reshape(1, width)
+    coming.value_bias.wait()
+    vectors[7:8, 2 * width : 3 * width] = held.value_bias[...].reshape(1, width)
+    first_gain, first_shift = vectors[0:1, :], vectors[1:2, :]
+    out_bias, second_gain = vectors[2:3, :], vectors[3:4, :]
+    second_shift, down_bias = vectors[4:5, :], vectors[5:6, :]
+    tokens_ref, cotangent_ref = held.tokens, held.cotangent
+    coming.tokens.wait()
+    coming.cotangent.wait()
+    token_rows = tokens_ref[...].astype(f32)
+    normed, hat, inv_scale = norm_rows(token_rows, first_gain, first_shift)
+    first_all[slot(near, c), :] = normed.astype(bf16)
+    ref.first_hat[...] = hat
+    ref.row_scale[0] = jnp.broadcast_to(inv_scale, (rows, LANES))
+
+    pl.semaphore_wait(barrier, len(peers))
+
+    first_sems = share_start(first_all)
+    lane_cut = round_up(qkv_lanes // 2, LANES)
+    q_parts = [(attn_w, 0, lane_cut), (attn_w, lane_cut, qkv_lanes)]
+    o_part = (attn_w, qkv_lanes, all_lanes)
+    q_base = [spread_start(attn_piece, *part) for part in q_parts]
+    o_base = spread_start(attn_piece, *o_part)
+    vec_sem = net.sem()
+    net.send(vectors, ref.far_vectors, dev_far, vec_sem)
+    up_parts = [
+        WideGather(ref.up_piece, up_w, ref.up_wait, lo, hi)
+        for lo, hi in row_cuts(piece, 2)
+    ]
+    down_parts = [
+        WideGather(ref.down_piece, down_w, ref.down_wait, lo, hi)
+        for lo, hi in row_cuts(piece, 3)
+    ]
+
+    for padded, copy, raw in (
+        (ref.up_piece, coming.up_w, held.up_w),
+        (ref.down_piece, coming.down_w, held.down_w),
+    ):
+        copy.wait()
+        padded[...] = jnp.zeros((piece, ff_lanes), bf16)
+        padded[:, :units] = raw[...]
+    dy_all[slot(near, kx), :] = cotangent_ref[...]
+    vec_own[5:6, :] = jnp.sum(cotangent_ref[...].astype(f32), axis=0, keepdims=True)
+    head_rows[...] = jnp.zeros_like(head_rows)
+    head_grads[...] = jnp.zeros_like(head_grads)
+    mixed_all[...] = jnp.zeros_like(mixed_all)
+    qkv_grads[...] = jnp.zeros_like(qkv_grads)
+
+    for part in up_parts:
+        part.start(inner)
+    dy_sems = plain_share_z(dy_all)
+    q_sems = [gather_start(*part, base) for part, base in zip(q_parts, q_base)]
+    for part in up_parts:
+        part.start(jnp.logical_and(outer, away))
+    for part, sems in zip(q_parts, q_sems):
+        gather_forward(*part, sems)
+    for part in up_parts:
+        part.start(jnp.logical_and(outer, home))
+    o_sems = gather_start(*o_part, o_base)
+    share_forward(first_all, first_sems)
+    net.arrived(ref.far_vectors, vec_sem)
+    share_near(first_all, first_sems)
+    share_deep(first_all, first_sems)
+    for part, sems in zip(q_parts, q_sems):
+        gather_finish(*part, sems)
+    down_parts[0].start(jnp.logical_or(inner, outer))
+    for part in down_parts[1:]:
+        part.start(inner)
+    gather_forward(*o_part, o_sems)
+    plain_share_x(dy_all, dy_sems)
+    for part in up_parts:
+        part.beside()
+    for part in down_parts:
+        part.beside()
+
+    def shard_vector(row, own):
+        return jnp.where(own, vectors[row : row + 1, :], ref.far_vectors[row : row + 1, :])
+
+    qkv_bias = shard_vector(7, home)[:, :qkv_lanes]
+    for side_at in range(2):
+        side_rows = slice(side_at * pair, (side_at + 1) * pair)
+        done = dot_plain(first_all[side_rows, :], attn_w[:, :qkv_lanes])
+        done = (done + qkv_bias).astype(bf16)
+        for image in range(2):
+            to = slice(image * pair + side_at * rows, image * pair + (side_at + 1) * rows)
+            for head in range(3 * heads):
+                head_rows[head, to, :HD] = done[
+                    image * rows : (image + 1) * rows, head * HD : (head + 1) * HD
+                ]
+    scale = HD ** (-0.5)
+
+    def image_head(step):
+        head, image = lax.rem(step, heads), lax.div(step, heads)
+        return head, aligned(image * pair, pair)
+
+    def attend(step, carry):
+        head, span = image_head(step)
+        queries, keys_part = head_rows[head, span, :], head_rows[heads + head, span, :]
+        values = head_rows[2 * heads + head, span, :]
+        scores = dot_right_t(queries, keys_part) * scale
+        expo = jnp.exp(scores - jnp.max(scores, axis=1, keepdims=True))
+        probs = expo / jnp.sum(expo, axis=1, keepdims=True)
+        ref.probs_all[step] = probs
+        mixed = dot_plain(probs.astype(bf16), values)
+        ref.mixed_heads[head, span, :] = mixed.astype(bf16)
+        return carry
+
+    lax.fori_loop(0, 2 * heads, attend, 0, unroll=2)
+
+    def pack(target, source, count, base):
+        for side_at in range(2):
+            for image in range(2):
+                at = slice(side_at * pair + image * rows, side_at * pair + (image + 1) * rows)
+                take = slice(image * pair + side_at * rows, image * pair + (side_at + 1) * rows)
+                for head in range(count):
+                    lo = base + head * HD
+                    target[at, lo : lo + HD] = source[head, take, :HD]
+
+    pack(mixed_all, ref.mixed_heads, heads, win_shift)
+
+    def half(side):
+        return aligned(side, pair)
+
+    gather_finish(*o_part, o_sems)
+    part_a[half(deep), :] = dot_right_t(mixed_all[half(deep), :], attn_w[:, win:])
+    out_sems = sum_deep(0, part_a)
+    part_a[half(near), :] = dot_right_t(mixed_all[half(near), :], attn_w[:, win:])
+    sum_pass(0, part_a, out_sems)
+    sum_near(0, part_a, out_sems)
+    for part in down_parts[1:]:
+        part.start(outer)
+    for part in up_parts:
+        part.second()
+    up_parts[0].third()
+    attn_rows = sum_finish(0, part_a, out_sems)
+    middle = tokens_ref[...].astype(f32) + attn_rows + out_bias
+    ref.mid_rows[...] = middle
+    normed, hat, inv_scale = norm_rows(middle, second_gain, second_shift)
+    second_all[slot(near, kx), :] = normed.astype(bf16)
+    ref.second_hat[...] = hat
+    ref.row_scale[1] = jnp.broadcast_to(inv_scale, (rows, LANES))
+    second_sems = wide_share_start(second_all)
+    up_parts[1].third()
+    wide_share_forward(second_all, second_sems)
+    for part in down_parts:
+        part.second()
+    plain_share_forward(dy_all, dy_sems)
+    for part in up_parts:
+        part.fourth()
+    down_parts[0].third()
+    for part in up_parts:
+        part.finish()
+    wide_share_near(second_all, second_sems)
+
+    up_bias = shard_vector(6, stay)
+    chunk = 32
+
+    def raise_half(side):
+        part_b[half(side), :] = dot_plain(second_all[half(side), :], up_w[...])
+
+        def gelu_rows(step, carry):
+            at = aligned(side + step * chunk, chunk)
+            value, slope = gelu_pair(part_b[at, :] + up_bias)
+            hidden_all[at, :] = value.astype(bf16)
+            slope_all[at, :] = slope
+            return carry
+
+        lax.fori_loop(0, pair // chunk, gelu_rows, 0)
+
+    raise_half(near)
+    down_parts[1].third()
+    wide_share_deep(second_all, second_sems)
+    raise_half(deep)
+
+    tile = 3 * LANES
+
+    def outer_product(grad, left, right, lo, hi):
+        def rows_of(step, carry):
+            at = aligned(step * tile, tile)
+            grad[at, lo:hi] = dot_left_t(left[:, at], right).astype(bf16)
+            return carry
+
+        lax.fori_loop(0, D // tile, rows_of, 0)
+
+    down_parts[2].third()
+    down_parts[0].fourth()
+    plain_share_finish(dy_all, dy_sems)
+    outer_product(down_g, dy_all, hidden_all[...], 0, ff_lanes)
+    down_reduce = wide_reduce_first(down_g, ref.land_d)
+    down_parts[1].fourth()
+    wide_reduce_second(down_g, ref.land_d, down_reduce)
+    down_parts[2].fourth()
+    for part in down_parts:
+        part.finish()
+
+    def lower_half(side):
+        part_b[half(side), :] = dot_plain(dy_all[half(side), :], down_w[...])
+
+        def slope_rows(step, total):
+            at = aligned(side + step * chunk, chunk)
+            low = (part_b[at, :] * slope_all[at, :]).astype(bf16)
+            upper_all[at, :] = low
+            return total + jnp.sum(low.astype(f32), axis=0, keepdims=True)
+
+        return lax.fori_loop(0, pair // chunk, slope_rows, jnp.zeros((1, ff_lanes), f32))
+
+    up_bias_sum = lower_half(deep)
+    part_a[half(deep), :] = dot_right_t(upper_all[half(deep), :], up_w[...])
+    second_sum_sems = wide_sum_deep(0, part_a)
+    up_bias_sum = up_bias_sum + lower_half(near)
+    vec_own[6:7, :] = up_bias_sum
+    part_a[half(near), :] = dot_right_t(upper_all[half(near), :], up_w[...])
+    wide_sum_near(0, part_a, second_sum_sems)
+    outer_product(up_g, second_all, upper_all[...], 0, ff_lanes)
+    up_reduce = wide_reduce_first(up_g, ref.land_u)
+    wide_sum_pass(0, part_a, second_sum_sems)
+    wide_reduce_second(up_g, ref.land_u, up_reduce)
+    wide_reduce_third(down_g, ref.land_d, down_reduce)
+    second_grad = wide_sum_finish(0, part_a, second_sum_sems)
+    back, gain_sum, shift_sum = norm_back(
+        second_grad, ref.second_hat[...], ref.row_scale[1][:, :1], second_gain
+    )
+    vec_own[3:4, :] = gain_sum[None, :]
+    vec_own[4:5, :] = shift_sum[None, :]
+    total = cotangent_ref[...].astype(f32) + back
+    ref.mid_grad[...] = total
+    low = total.astype(bf16)
+    mid_all[slot(near, c), :] = low
+    vec_own[2:3, :] = jnp.sum(low.astype(f32), axis=0, keepdims=True)
+    mid_sems = share_start(mid_all)
+    part_b[half(deep), :] = dot_right_t(hidden_all[half(deep), :], down_w[...])
+    mlp_sems = wide_sum_deep(1, part_b)
+    part_b[half(near), :] = dot_right_t(hidden_all[half(near), :], down_w[...])
+    wide_sum_near(1, part_b, mlp_sems)
+    def head_half(side_at):
+        side_rows = slice(side_at * pair, (side_at + 1) * pair)
+        done = dot_plain(mid_all[side_rows, :], attn_w[:, win:]).astype(bf16)
+        for image in range(2):
+            to = slice(image * pair + side_at * rows, image * pair + (side_at + 1) * rows)
+            for head in range(heads):
+                lo = win_shift + head * HD
+                head_grads[head, to, :HD] = done[image * rows : (image + 1) * rows, lo : lo + HD]
+
+    share_forward(mid_all, mid_sems)
+    share_near(mid_all, mid_sems)
+    wide_reduce_cross(down_g, ref.land_d, down_reduce)
+    wide_reduce_fourth(down_g, ref.land_d, down_reduce)
+    share_deep(mid_all, mid_sems)
+    head_half(0)
+    head_half(1)
+    wide_reduce_third(up_g, ref.land_u, up_reduce)
+    wide_reduce_cross(up_g, ref.land_u, up_reduce)
+
+    cut = round_up(2 * width, LANES)
+
+    def value_back(step, carry):
+        head, span = image_head(step)
+        low = ref.probs_all[step].astype(bf16)
+        value_grad = dot_left_t(low, head_grads[head, span, :])
+        ref.mixed_heads[head, span, :] = value_grad.astype(bf16)
+        return carry
+
+    def value_out_rows(step, carry):
+        at = aligned(step * tile, tile)
+        by_value = dot_left_t(first_all[:, at], qkv_grads[:, cut:qkv_lanes])
+        by_out = dot_left_t(mid_all[:, at], mixed_all[...])
+        both = by_value[:, win - cut :] + by_out[:, :skip]
+        attn_g[at, cut:win] = by_value[:, : win - cut].astype(bf16)
+        attn_g[at, win:qkv_lanes] = both.astype(bf16)
+        attn_g[at, qkv_lanes:] = by_out[:, skip:].astype(bf16)
+        return carry
+
+    lax.fori_loop(0, 2 * heads, value_back, 0, unroll=2)
+    pack(qkv_grads, ref.mixed_heads, heads, 2 * width)
+    lax.fori_loop(0, D // tile, value_out_rows, 0)
+    vo_args = attn_g, ref.land_vo, cut, all_lanes, net.sems(10)
+    reduce_first(*vo_args)
+
+    def attend_back(step, carry):
+        head, span = image_head(step)
+        queries, keys_part = head_rows[head, span, :], head_rows[heads + head, span, :]
+        values, grads = head_rows[2 * heads + head, span, :], head_grads[head, span, :]
+        probs = ref.probs_all[step]
+        prob_grad = dot_right_t(grads, values)
+        row_dot = jnp.sum(probs * prob_grad, axis=1, keepdims=True)
+        score_grad = (probs * (prob_grad - row_dot)).astype(bf16)
+        query_grad = dot_plain(score_grad, keys_part) * scale
+        key_grad = dot_left_t(score_grad, queries) * scale
+        head_rows[head, span, :] = query_grad.astype(bf16)
+        head_rows[heads + head, span, :] = key_grad.astype(bf16)
+        return carry
+
+    lax.fori_loop(0, 2 * heads, attend_back, 0, unroll=2)
+    pack(qkv_grads, head_rows, 2 * heads, 0)
+    wide_reduce_fourth(up_g, ref.land_u, up_reduce)
+    outer_product(attn_g, first_all, qkv_grads[:, :cut], 0, cut)
+    qk_args = attn_g, ref.land_qk, 0, cut, net.sems(10)
+    reduce_first(*qk_args, when=away)
+    part_a[half(deep), :] = dot_right_t(
+        qkv_grads[half(deep), :qkv_lanes], attn_w[:, :qkv_lanes]
+    )
+    first_sum_sems = sum_deep(1, part_a)
+    part_a[half(near), :] = dot_right_t(
+        qkv_grads[half(near), :qkv_lanes], attn_w[:, :qkv_lanes]
+    )
+    sum_pass(1, part_a, first_sum_sems)
+    sum_near(1, part_a, first_sum_sems)
+    reduce_first(*qk_args, when=home)
+    vec_own[7:8, :] = jnp.sum(qkv_grads[...].astype(f32), axis=0, keepdims=True)
+    reduce_second(*vo_args)
+    wide_sum_pass(1, part_b, mlp_sems)
+    reduce_second(*qk_args, when=away)
+    first_grad = sum_finish(1, part_a, first_sum_sems)
+    back, gain_sum, shift_sum = norm_back(
+        first_grad, ref.first_hat[...], ref.row_scale[0][:, :1], first_gain
+    )
+    vec_own[0:1, :] = gain_sum[None, :]
+    vec_own[1:2, :] = shift_sum[None, :]
+    vec_sems = vector_planes()
+    ref.mid_grad[...] = ref.mid_grad[...] + back
+    store(ref.mid_grad, out.input_grad)
+    reduce_third(*vo_args)
+    reduce_second(*qk_args, when=home)
+    reduce_third(*qk_args)
+    vec_sems = vector_chips(vec_sems)
+    ref.down_buf[...] = wide_reduce_finish(down_g, ref.land_d, down_reduce)
+    store(ref.down_buf, out.down_grad)
+    vec_sems = vector_core(vec_sems)
+    mlp_rows = wide_sum_finish(1, part_b, mlp_sems)
+    ref.layer_buf[...] = (ref.mid_rows[...] + mlp_rows + down_bias).astype(bf16)
+    store(ref.layer_buf, out.layer_out)
+    vector_finish(vec_sems)
+    store(ref.vec_done, out.vector_grad)
+    ref.up_buf[...] = wide_reduce_finish(up_g, ref.land_u, up_reduce)
+    store(ref.up_buf, out.up_grad)
+    ref.attn_buf[:, cut:] = reduce_finish(ref.land_vo, vo_args[4])
+    ref.attn_buf[:, :cut] = reduce_finish(ref.land_qk, qk_args[4])
+    store(ref.attn_buf, out.attn_grad)
+    net.drain()
+    assert net.used <= ref.send_sems.shape[0]
+    for copy in stores:
+        copy.wait()
+
+
+def format_kernel(shapes, *refs):
+    width, units = shapes
+    inputs, refs = refs[:6], refs[6:]
+    outs, refs = refs[:17], refs[17:]
+    held, refs = refs[:6], refs[6:]
+    shaped, sems = refs[:-1], refs[-1]
+    copies = [
+        pltpu.make_async_copy(source, target, sems.at[number])
+        for number, (source, target) in enumerate(zip(inputs, held, strict=True))
+    ]
+    for copy in copies:
+        copy.start()
+    going = []
+
+    def put(source, number):
+        copy = pltpu.make_async_copy(source, outs[number], sems.at[6 + number])
+        copy.start()
+        going.append(copy)
+
+    def put_shaped(number, value):
+        shaped[number - 2][...] = value
+        put(shaped[number - 2], number)
+
+    copies[0].wait()
+    put(held[0], 0)
+    copies[1].wait()
+    put(held[1], 1)
+    copies[2].wait()
+    for number, place in ((4, 0), (5, 1), (6, 2), (9, 3)):
+        put_shaped(number, held[2][:, place * width : (place + 1) * width])
+    copies[3].wait()
+    put_shaped(13, held[3][:, :units])
+    copies[4].wait()
+    put_shaped(15, held[4][:, :units])
+    copies[5].wait()
+    for number, row, lo, size in (
+        (2, 0, 0, D),
+        (3, 1, 0, D),
+        (10, 2, 0, D),
+        (11, 3, 0, D),
+        (12, 4, 0, D),
+        (16, 5, 0, D),
+        (14, 6, 0, units),
+        (7, 7, 0, width),
+        (8, 7, 2 * width, width),
+    ):
+        put_shaped(number, held[5][row, lo : lo + size])
+    for copy in going:
+        copy.wait()
+
+
+def fused_step(
+    tokens,
+    cotangent,
+    first_gain,
+    first_shift,
+    query_weight,
+    key_weight,
+    value_weight,
+    query_bias,
+    value_bias,
+    out_weight,
+    out_bias,
+    second_gain,
+    second_shift,
+    up_weight,
+    up_bias,
+    down_weight,
+    down_bias,
+):
+    bf16, f32 = jnp.bfloat16, jnp.float32
+    rows, piece, width, units = (
+        tokens.shape[0],
+        query_weight.shape[0],
+        query_weight.shape[1],
+        up_weight.shape[1],
+    )
+    heads = width // HD
+    group = 4 * rows
+    qkv_lanes = round_up(3 * width, LANES)
+    attn_lanes = round_up(4 * width, LANES)
+    ff_lanes = round_up(units, LANES)
+    win = 3 * width // LANES * LANES
+    given = dict(
+        query_w=query_weight,
+        key_w=key_weight,
+        value_w=value_weight,
+        out_w=out_weight.T,
+        first_gain=first_gain,
+        first_shift=first_shift,
+        out_bias=out_bias,
+        second_gain=second_gain,
+        second_shift=second_shift,
+        down_bias=down_bias,
+        up_bias=up_bias,
+        query_bias=query_bias,
+        value_bias=value_bias,
+        tokens=tokens,
+        cotangent=cotangent,
+        up_w=up_weight,
+        down_w=down_weight.T,
+    )
+    place = pl.BlockSpec(memory_space=pl.ANY)
+    sem_count = 148
+    cut = round_up(2 * width, LANES)
+    raw_outs = dict(
+        layer_out=jax.ShapeDtypeStruct((rows, D), bf16),
+        input_grad=jax.ShapeDtypeStruct((rows, D), f32),
+        attn_grad=jax.ShapeDtypeStruct((piece, attn_lanes), f32),
+        up_grad=jax.ShapeDtypeStruct((piece, ff_lanes), f32),
+        down_grad=jax.ShapeDtypeStruct((piece, ff_lanes), f32),
+        vector_grad=jax.ShapeDtypeStruct((8, D), f32),
+    )
+    scratch = dict(
+        attn_piece=pltpu.VMEM((piece, attn_lanes), bf16),
+        up_piece=pltpu.VMEM((piece, ff_lanes), bf16),
+        down_piece=pltpu.VMEM((piece, ff_lanes), bf16),
+        up_wait=pltpu.VMEM((piece, ff_lanes), bf16),
+        down_wait=pltpu.VMEM((piece, ff_lanes), bf16),
+        attn_w=pltpu.VMEM((D, attn_lanes), bf16),
+        up_w=pltpu.VMEM((D, ff_lanes), bf16),
+        down_w=pltpu.VMEM((D, ff_lanes), bf16),
+        attn_g=pltpu.VMEM((D, attn_lanes), bf16),
+        up_g=pltpu.VMEM((D, ff_lanes), bf16),
+        down_g=pltpu.VMEM((D, ff_lanes), bf16),
+        land_vo=pltpu.VMEM((8, piece, attn_lanes - cut), bf16),
+        land_qk=pltpu.VMEM((8, piece, cut), bf16),
+        land_u=pltpu.VMEM((8, piece, ff_lanes), bf16),
+        land_d=pltpu.VMEM((8, piece, ff_lanes), bf16),
+        first_all=pltpu.VMEM((group, D), bf16),
+        second_all=pltpu.VMEM((group, D), bf16),
+        dy_all=pltpu.VMEM((group, D), bf16),
+        mid_all=pltpu.VMEM((group, D), bf16),
+        head_rows=pltpu.VMEM((3 * heads, group, LANES), bf16),
+        head_grads=pltpu.VMEM((heads, group, LANES), bf16),
+        probs_all=pltpu.VMEM((2 * heads, 2 * rows, 2 * rows), f32),
+        mixed_heads=pltpu.VMEM((heads, group, LANES), bf16),
+        mixed_all=pltpu.VMEM((group, attn_lanes - win), bf16),
+        hidden_all=pltpu.VMEM((group, ff_lanes), bf16),
+        slope_all=pltpu.VMEM((group, ff_lanes), f32),
+        upper_all=pltpu.VMEM((group, ff_lanes), bf16),
+        qkv_grads=pltpu.VMEM((group, attn_lanes), bf16),
+        part_a=pltpu.VMEM((group, D), f32),
+        part_b=pltpu.VMEM((group, D), f32),
+        core_send=pltpu.VMEM((2, 2, rows, D), bf16),
+        core_land=pltpu.VMEM((2, 2, rows, D), bf16),
+        deep_send=pltpu.VMEM((2, rows, D), bf16),
+        deep_land=pltpu.VMEM((2, rows, D), bf16),
+        wide_send=pltpu.VMEM((2, 6, rows // 2, D), bf16),
+        wide_land=pltpu.VMEM((2, 6, rows // 2, D), bf16),
+        first_hat=pltpu.VMEM((rows, D), f32),
+        second_hat=pltpu.VMEM((rows, D), f32),
+        mid_rows=pltpu.VMEM((rows, D), f32),
+        mid_grad=pltpu.VMEM((rows, D), f32),
+        row_scale=pltpu.VMEM((2, rows, LANES), f32),
+        vectors=pltpu.VMEM((8, D), f32),
+        far_vectors=pltpu.VMEM((8, D), f32),
+        vec_own=pltpu.VMEM((8, D), f32),
+        by_plane=pltpu.VMEM((4, 8, D), f32),
+        vec_chip=pltpu.VMEM((8, D), f32),
+        by_chip=pltpu.VMEM((4, 8, D), f32),
+        vec_core=pltpu.VMEM((8, D), f32),
+        vec_core_land=pltpu.VMEM((8, D), f32),
+        vec_done=pltpu.VMEM((8, D), f32),
+        layer_buf=pltpu.VMEM((rows, D), bf16),
+        attn_buf=pltpu.VMEM((piece, attn_lanes), f32),
+        up_buf=pltpu.VMEM((piece, ff_lanes), f32),
+        down_buf=pltpu.VMEM((piece, ff_lanes), f32),
+        load_sems=pltpu.SemaphoreType.DMA((len(given) + len(raw_outs),)),
+        send_sems=pltpu.SemaphoreType.DMA((sem_count,)),
+        recv_sems=pltpu.SemaphoreType.DMA((sem_count,)),
+    )
+    shapes = (rows, heads, width, units, qkv_lanes, piece)
+    names = tuple(given), tuple(raw_outs), tuple(scratch)
+
+    def body(*refs):
+        layer_kernel(shapes, names, *refs)
+
+    raw = pl.pallas_call(
+        body,
+        out_shape=tuple(raw_outs.values()),
+        in_specs=[place] * len(given),
+        out_specs=(place,) * len(raw_outs),
+        scratch_shapes=[
+            *(pltpu.VMEM(array.shape, array.dtype) for array in given.values()),
+            *scratch.values(),
+        ],
+        compiler_params=pltpu.CompilerParams(
+            collective_id=0, has_side_effects=True, vmem_limit_bytes=67043328
+        ),
+        name="layer",
+    )(*given.values())
+    raw_outs = tuple(raw_outs.values())
+
+    vector, narrow = jax.ShapeDtypeStruct((D,), f32), jax.ShapeDtypeStruct((width,), f32)
+    attn_out = jax.ShapeDtypeStruct((piece, width), f32)
+    ff_out = jax.ShapeDtypeStruct((piece, units), f32)
+    outs = (
+        *raw_outs[:2],
+        vector,
+        vector,
+        attn_out,
+        attn_out,
+        attn_out,
+        narrow,
+        narrow,
+        attn_out,
+        vector,
+        vector,
+        vector,
+        ff_out,
+        jax.ShapeDtypeStruct((units,), f32),
+        ff_out,
+        vector,
+    )
+
+    def format_body(*refs):
+        format_kernel((width, units), *refs)
+
+    done = pl.pallas_call(
+        format_body,
+        out_shape=outs,
+        in_specs=[place] * 6,
+        out_specs=(place,) * 17,
+        scratch_shapes=[
+            *(pltpu.VMEM(item.shape, item.dtype) for item in raw_outs),
+            *(pltpu.VMEM(item.shape, item.dtype) for item in outs[2:]),
+            pltpu.SemaphoreType.DMA((6 + 17,)),
+        ],
+        compiler_params=pltpu.CompilerParams(vmem_limit_bytes=67043328),
+        name="outputs",
+    )(*raw)
+    done = list(done)
+    done[9], done[15] = done[9].T, done[15].T
+    return tuple(done)
+
+
+def pick_step(mesh):
+    if mesh.shape["fsdp"] == 8 and mesh.shape["tensor"] == 4:
+        return fused_step
+    return on_device
+
+
 def solution(mesh):
     return jax.shard_map(
-        on_device,
+        pick_step(mesh),
         mesh=mesh,
         in_specs=(
             P(("fsdp", "tensor"), None),

time: 678 us -> 162 us (0.24)
  waiting for transfers between devices: 482 us -> 0 us
  Pallas kernels: 0 us -> 161 us
  blocking collectives: 88.1 us -> 0 us
  matrix products: 52 us -> 0 us
  local copies, waits for them, and re-layouts: 21.5 us -> 0 us
  other arithmetic: 15.7 us -> 0 us
  between operations: 16.1 us -> 0.85 us
    reduce_scatter x7 -> x0, waiting for transfers between devices: 236 us -> none  [the longest x1 61.3 us: on_device(): lax.psum_scatter(up_grad, 'fsdp', scatter_dimension=0, tiled=True)]
    pallas_call x0 -> x2, Pallas kernels: none -> 161 us  [the longest x1 158 us: fused_step(): pl.pallas_call(body, out_shape=tuple(raw_outs.values()), in_specs=[place]...]
    unnamed x19 -> x0, waiting for transfers between devices: 132 us -> none
    all_gather x6 -> x0, waiting for transfers between devices: 114 us -> none  [the longest x1 32.2 us: on_device(): lax.all_gather(down_weight, 'fsdp', axis=1, tiled=True)]
    dot_general x18 -> x0, matrix products: 52 us -> none  [the longest x4 17.9 us: dot_plain(): return jnp.dot(left, right, preferred_element_type=jnp.float32)]
    all_gather x4 -> x0, blocking collectives: 46.7 us -> none  [the longest x1 14 us: on_device(): lax.all_gather(query_weight, 'fsdp', axis=0, tiled=True)]
    psum x1 -> x0, blocking collectives: 41.4 us -> none  [on_device(): lax.psum((small_terms, head_terms), ('fsdp', 'tensor'))]
    unnamed x70 -> x0, local copies, waits for them, and re-layouts: 14.1 us -> none
  transfers between devices with their start and end apart: 16 -> 0, of which waited for: 13 -> 0; matrix products, arithmetic and copies ran while one was open for 7% -> 0% of each run, Pallas kernels for 0% -> 0%
where the time goes in v2:
time: 162 us
  Pallas kernels  161 us (99%)
    pallas_call x1, Pallas kernels, fused_step(): pl.pallas_call(body, out_shape=tuple(raw_outs.values()), in_specs=[place]...  158 us

profile of v2, /device:TPU:1, one launch (start us, length us, event | category | flops | bytes accessed | tf_op | source)
XLA Modules:
  0.0 161.8 jit_solution(3409652690806715618)
XLA Ops:
  0.7 157.9 %layer.1 = (bf16[128,1152]{1,0:T(8,128)(2,1)}, f32[128,1152]{1,0:T(8,128)}, f32[144,1152]{1,0:T(8,128)}, f32[144,1152]{1,0:T(8,128)}, f32[144,1152]{1,0:T(8,128)}, /*index=5*/f32[8,1152]{1,0:T(8,128)}) custom-call(bf16[144,288]{1,0:T(8,128)(2,1)} %refs_0_.1, bf16[144,288]{1,0:T(8,128)(2,1)} %refs_1_.1, bf16[144,288]{1,0:T(8,128)(2,1)} %refs_2_.1, ...), custom_call_target="tpu_custom_call" | custom-call | tf_op jit(solution)/shard_map/layer/pallas_call | solution.py:1336
  158.5 3.1 %outputs.1 = (bf16[128,1152]{1,0:T(8,128)(2,1)}, f32[128,1152]{1,0:T(8,128)}, f32[1152]{0:T(1024)}, f32[1152]{0:T(1024)}, f32[144,288]{1,0:T(8,128)}, /*index=5*...) custom-call(bf16[128,1152]{1,0:T(8,128)(2,1)} %get-tuple-element.40., ...), custom_call_target="tpu_custom_call" | custom-call | tf_op jit(solution)/shard_map/outputs/pallas_call | solution.py:1377

commit v3 on v2

--- a/solution.py
+++ b/solution.py
@@ -302,7 +302,8 @@
     def __init__(self, send_sems, recv_sems):
         self.send_sems, self.recv_sems = send_sems, recv_sems
         self.used = 0
-        self.pending = []
+        self.sent = 0
+        self.slots = [None] * send_sems.shape[0]
 
     def sem(self):
         self.used += 1
@@ -311,34 +312,43 @@
     def sems(self, count):
         return [self.sem() for _ in range(count)]
 
-    def send(self, src, dst, device, sem, recv=None, when=None):
+    def release(self, slot):
+        if self.slots[slot] is not None:
+            copy, when = self.slots[slot]
+            guarded(when, copy.wait_send)
+
+    def send(self, src, dst, device, recv, when=None):
+        slot = self.sent % len(self.slots)
+        self.sent += 1
+        self.release(slot)
         copy = pltpu.make_async_remote_copy(
             src_ref=src,
             dst_ref=dst,
-            send_sem=self.send_sems.at[sem],
-            recv_sem=self.recv_sems.at[sem if recv is None else recv],
+            send_sem=self.send_sems.at[slot],
+            recv_sem=self.recv_sems.at[recv],
             device_id=device,
             device_id_type=MESH_IDS,
         )
-        if when is None:
-            copy.start()
-        else:
-            pl.when(when)(copy.start)
-        self.pending.append((copy, when))
+        guarded(when, copy.start)
+        self.slots[slot] = copy, when
 
     def local(self, src, dst, sem, when):
         copy = pltpu.make_async_copy(src, dst, self.recv_sems.at[sem])
-        pl.when(when)(copy.start)
+        guarded(when, copy.start)
 
     def arrived(self, dst, sem):
         pltpu.make_async_copy(dst, dst, self.recv_sems.at[sem]).wait()
 
     def drain(self):
-        for copy, when in self.pending:
-            if when is None:
-                copy.wait_send()
-            else:
-                pl.when(when)(copy.wait_send)
+        for slot in range(len(self.slots)):
+            self.release(slot)
+
+
+def guarded(when, action):
+    if when is None:
+        action()
+    else:
+        pl.when(when)(action)
 
 
 def layer_kernel(shapes, names, *refs):
@@ -366,6 +376,8 @@
     win_shift = out_base - win
     skip = qkv_lanes - win
     all_lanes, ff_lanes = attn_w.shape[1], up_w.shape[1]
+    main = units // LANES * LANES
+    rest = units - main
 
     f = lax.axis_index("fsdp")
     t = lax.axis_index("tensor")
@@ -404,38 +416,35 @@
         return aligned(side + place * rows, rows)
 
     def spread_start(src, buf, lo, hi):
-        base, other = net.sems(2)
+        base, _ = net.sems(2)
         source, target = src.at[:, lo:hi], block(buf, f, lo, hi)
         net.local(source, target, base + c, home)
         to = {"fsdp": 2 * k + zh, "tensor": t}
-        net.send(source, target, to, base, recv=base + c, when=away)
+        net.send(source, target, to, base + c, when=away)
         to = {"fsdp": 2 * k + zh, "tensor": far_t}
-        net.send(source, target, to, other, recv=base + c)
+        net.send(source, target, to, base + c)
         return base
 
     def gather_start(buf, lo, hi, base):
-        sems = net.sems(6)
+        sems = net.sems(3)
         a_own, b_own = block(buf, 2 * k, lo, hi), block(buf, 2 * k + 1, lo, hi)
         net.arrived(a_own, base)
         net.send(a_own, a_own, dev_x, sems[0])
         net.arrived(b_own, base + 1)
         net.send(b_own, b_own, dev_y, sems[1])
         net.send(a_own, a_own, dev_y, sems[2])
-        net.send(b_own, b_own, dev_x, sems[3])
+        net.send(b_own, b_own, dev_x, sems[2])
         return sems
 
     def gather_forward(buf, lo, hi, sems):
         a_x, b_y = block(buf, 2 * k_x, lo, hi), block(buf, 2 * k_y + 1, lo, hi)
         net.arrived(a_x, sems[0])
-        net.send(a_x, a_x, dev_y, sems[4])
+        net.send(a_x, a_x, dev_y, sems[2])
         net.arrived(b_y, sems[1])
-        net.send(b_y, b_y, dev_x, sems[5])
+        net.send(b_y, b_y, dev_x, sems[2])
 
     def gather_finish(buf, lo, hi, sems):
-        net.arrived(block(buf, 2 * k_y, lo, hi), sems[2])
-        net.arrived(block(buf, 2 * k_x + 1, lo, hi), sems[3])
-        net.arrived(block(buf, 2 * k_d, lo, hi), sems[4])
-        net.arrived(block(buf, 2 * k_d + 1, lo, hi), sems[5])
+        net.arrived(buf.at[0 : 4 * piece, lo:hi], sems[2])
 
     f_x, f_y, f_d = 2 * k_x + c, 2 * k_y + c, 2 * k_d + c
 
@@ -443,7 +452,7 @@
         def __init__(self, src, buf, wait_at, lo, hi):
             self.buf, self.lo, self.size = buf, lo, hi - lo
             self.src, self.wait_at = src.at[lo:hi, :], wait_at.at[lo:hi, :]
-            self.sems = net.sems(9)
+            self.sems = net.sems(6)
 
         def at(self, index):
             start = pl.multiple_of(index * piece + self.lo, 16)
@@ -452,7 +461,7 @@
         def start(self, when):
             own, sems = self.at(f), self.sems
             stay_now, move_now = jnp.logical_and(stay, when), jnp.logical_and(move, when)
-            net.local(self.src, own, sems[8], stay_now)
+            net.local(self.src, own, sems[4], stay_now)
             net.send(self.src, own, dev_far, sems[0], when=stay_now)
             net.send(self.src, self.wait_at, dev_far, sems[0], when=move_now)
 
@@ -474,26 +483,25 @@
 
             @pl.when(stay)
             def _():
-                net.arrived(own, sems[8])
+                net.arrived(own, sems[4])
 
             net.send(own, own, dev_y, sems[2])
-            net.send(own, own, dev_c, sems[4])
+            net.send(own, own, dev_c, sems[3])
 
         def third(self):
             got = self.at(f_x)
             net.arrived(got, self.sems[1])
-            net.send(got, got, dev_y, self.sems[3])
-            net.send(got, got, dev_c, self.sems[5])
+            net.send(got, got, dev_y, self.sems[5])
+            net.send(got, got, dev_c, self.sems[3])
 
         def fourth(self):
-            for index, sem, to in ((f_y, 2, 6), (f_d, 3, 7)):
+            for index, sem in ((f_y, 2), (f_d, 5)):
                 got = self.at(index)
                 net.arrived(got, self.sems[sem])
-                net.send(got, got, dev_c, self.sems[to])
+                net.send(got, got, dev_c, self.sems[3])
 
         def finish(self):
-            for index, sem in ((f, 4), (f_x, 5), (f_y, 6), (f_d, 7)):
-                net.arrived(self.at(index + oc - c), self.sems[sem])
+            net.arrived(self.buf.at[0 : 4 * self.size, :], self.sems[3])
 
     def share_start(buf):
         sems = net.sems(3)
@@ -542,28 +550,26 @@
         return aligned(side + place * rows + which * fourth, fourth)
 
     def wide_share_start(buf):
-        sems = net.sems(6)
+        sems = net.sems(4)
         first, second = buf.at[quarter(near, kx, 0)], buf.at[quarter(near, kx, 1)]
         net.send(first, first, dev_z, sems[0])
         net.send(second, second, dev_x, sems[1])
-        net.send(second, second, dev_z, sems[2])
-        net.send(first, first, dev_x, sems[3])
+        net.send(second, second, dev_z, sems[3])
+        net.send(first, first, dev_x, sems[2])
         return sems
 
     def wide_share_forward(buf, sems):
         from_z, from_x = buf.at[quarter(deep, kx, 0)], buf.at[quarter(near, ox, 1)]
         net.arrived(from_z, sems[0])
-        net.send(from_z, from_z, dev_x, sems[4])
+        net.send(from_z, from_z, dev_x, sems[3])
         net.arrived(from_x, sems[1])
-        net.send(from_x, from_x, dev_z, sems[5])
+        net.send(from_x, from_x, dev_z, sems[3])
 
     def wide_share_near(buf, sems):
-        net.arrived(buf.at[quarter(near, ox, 0)], sems[3])
+        net.arrived(buf.at[quarter(near, ox, 0)], sems[2])
 
     def wide_share_deep(buf, sems):
-        net.arrived(buf.at[quarter(deep, kx, 1)], sems[2])
-        net.arrived(buf.at[quarter(deep, ox, 0)], sems[4])
-        net.arrived(buf.at[quarter(deep, ox, 1)], sems[5])
+        net.arrived(buf.at[0 : 3 * fourth, :], sems[3])
 
     def plain_share_z(buf):
         sems = net.sems(3)
@@ -629,12 +635,6 @@
         total = grad[at, lo:hi].astype(f32) + land[...].astype(f32)
         grad[at, lo:hi] = total.astype(bf16)
 
-    def guarded(when, action):
-        if when is None:
-            action()
-        else:
-            pl.when(when)(action)
-
     def reduce_route(core, by_y):
         if core == 0 or by_y:
             return dev_y, 2 * k_y + core, 2 * k_x + core, dev_x
@@ -664,17 +664,24 @@
         for core in range(2):
             collect(2 * k + core, 2 * core)
 
-    def reduce_third(grad, land, lo, hi, sems):
+    def reduce_third(grad, land, lo, hi, sems, when=None):
+        def here(condition):
+            return condition if when is None else jnp.logical_and(when, condition)
+
         for core in range(2):
-            net.arrived(land.at[4 + core], sems[4 + core])
-            add_into(grad, 2 * k + core, lo, hi, land.at[4 + core])
+
+            def collect(core=core):
+                net.arrived(land.at[4 + core], sems[4 + core])
+                add_into(grad, 2 * k + core, lo, hi, land.at[4 + core])
+
+            guarded(when, collect)
             source = block(grad, 2 * k + core, lo, hi)
             mine, other = jnp.logical_and(home, c == core), jnp.logical_and(home, c != core)
-            net.local(source, land.at[6], sems[6], mine)
+            net.local(source, land.at[6], sems[6], here(mine))
             to = {"fsdp": 2 * k + core, "tensor": t}
-            net.send(source, land.at[6], to, sems[8], recv=sems[6], when=other)
+            net.send(source, land.at[6], to, sems[6], when=here(other))
             to = {"fsdp": 2 * k + core, "tensor": far_t}
-            net.send(source, land.at[7], to, sems[6 + core], recv=sems[7], when=away)
+            net.send(source, land.at[7], to, sems[7], when=here(away))
 
     def reduce_finish(land, sems):
         net.arrived(land.at[6], sems[6])
@@ -682,37 +689,40 @@
         return land[6].astype(f32) + land[7].astype(f32)
 
     def wide_reduce_first(grad, land):
-        sems = net.sems(8)
-        for number, index in enumerate((f_y, f_d, f, f_x)):
-            net.send(block(grad, index + oc - c), land.at[number], dev_c, sems[number])
+        sems = net.sems(6)
+        for number, index in enumerate((f_d, f_y, f, f_x)):
+            sem = sems[0] if number < 2 else sems[1]
+            net.send(block(grad, index + oc - c), land.at[number], dev_c, sem)
         return sems
 
     def wide_reduce_second(grad, land, sems):
-        for number, index in enumerate((f_y, f_d)):
-            net.arrived(land.at[number], sems[number])
-            add_into(grad, index, 0, ff_lanes, land.at[number])
+        net.arrived(land.at[0:2], sems[0])
+        for number, index in enumerate((f_d, f_y)):
+            add_into(grad, index, 0, grad.shape[1], land.at[number])
             net.send(block(grad, index), land.at[4 + number], dev_y, sems[4 + number])
+        net.arrived(land.at[2:4], sems[1])
         for number, index in ((2, f), (3, f_x)):
-            net.arrived(land.at[number], sems[number])
-            add_into(grad, index, 0, ff_lanes, land.at[number])
+            add_into(grad, index, 0, grad.shape[1], land.at[number])
 
     def wide_reduce_third(grad, land, sems):
+        net.arrived(land.at[4], sems[4])
+        add_into(grad, f_x, 0, grad.shape[1], land.at[4])
+        net.send(block(grad, f_x), land.at[6], dev_x, sems[2])
         net.arrived(land.at[5], sems[5])
-        add_into(grad, f_x, 0, ff_lanes, land.at[5])
-        net.send(block(grad, f_x), land.at[6], dev_x, sems[6])
-        net.arrived(land.at[4], sems[4])
-        add_into(grad, f, 0, ff_lanes, land.at[4])
-
-    def wide_reduce_cross(grad, land, sems):
-        net.send(block(grad, f), land.at[7], dev_far, sems[7], when=move)
-
-    def wide_reduce_fourth(grad, land, sems):
-        net.arrived(land.at[6], sems[6])
-        net.send(land.at[6], land.at[7], dev_far, sems[7], when=stay)
+        add_into(grad, f, 0, grad.shape[1], land.at[5])
+
+    def wide_reduce_cross(grad, land, sems, when):
+        now = jnp.logical_and(move, when)
+        net.send(block(grad, f), land.at[7], dev_far, sems[3], when=now)
+
+    def wide_reduce_fourth(grad, land, sems, when):
+        guarded(when, lambda: net.arrived(land.at[6], sems[2]))
+        now = jnp.logical_and(stay, when)
+        net.send(land.at[6], land.at[7], dev_far, sems[3], when=now)
 
     def wide_reduce_finish(grad, land, sems):
         kept = jnp.where(stay, grad[piece_at(f), :].astype(f32), land[6].astype(f32))
-        net.arrived(land.at[7], sems[7])
+        net.arrived(land.at[7], sems[3])
         return kept + land[7].astype(f32)
 
     vec_own, by_plane, by_chip = ref.vec_own, ref.by_plane, ref.by_chip
@@ -721,28 +731,26 @@
 
     def vector_planes():
         by_plane[t] = vec_own[...]
-        sems = net.sems(3)
-        for sem, plane in zip(sems, plane_peers, strict=True):
+        sem = net.sem()
+        for plane in plane_peers:
             net.send(vec_own, by_plane.at[t], {"fsdp": f, "tensor": plane}, sem)
-        return sems
-
-    def vector_chips(sems):
-        for sem, step in zip(sems, range(3, 0, -1), strict=True):
-            net.arrived(by_plane.at[lax.rem(t + step, 4)], sem)
+        return sem
+
+    def vector_chips(sem):
+        net.arrived(by_plane.at[0:3], sem)
         both = ref.vec_chip
         total = by_plane[0] + by_plane[1] + by_plane[2] + by_plane[3]
         shard = by_plane[zl] + by_plane[2 + zl]
         both[0:6, :] = total[0:6, :]
         both[6:8, :] = shard[6:8, :]
         by_chip[k] = both[...]
-        sems = net.sems(3)
-        for sem, chip in zip(sems, chip_peers, strict=True):
+        sem = net.sem()
+        for chip in chip_peers:
             net.send(both, by_chip.at[k], {"fsdp": 2 * chip + c, "tensor": t}, sem)
-        return sems
-
-    def vector_core(sems):
-        for sem, step in zip(sems, range(3, 0, -1), strict=True):
-            net.arrived(by_chip.at[lax.rem(k + step, 4)], sem)
+        return sem
+
+    def vector_core(sem):
+        net.arrived(by_chip.at[0:3], sem)
         held = ref.vec_core
         total = by_chip[0] + by_chip[1] + by_chip[2] + by_chip[3]
         units_total = by_chip[zh] + by_chip[2 + zh]
@@ -760,9 +768,7 @@
         done[7:8, :] = jnp.where(home, held[7:8, :], land[7:8, :])
 
     barrier = pltpu.get_barrier_semaphore()
-    dev_d = {"fsdp": 2 * k_d + c, "tensor": t}
-    dev_last = {"fsdp": f, "tensor": (1 - zh) * 2 + (1 - zl)}
-    peers = (dev_x, dev_y, dev_d, dev_c, dev_z, dev_far, dev_last, dev_far_other)
+    peers = (dev_x, dev_y, dev_c, dev_z, dev_far, dev_far_other)
     for peer in peers:
         pl.semaphore_signal(barrier, inc=1, device_id=peer, device_id_type=MESH_IDS)
 
@@ -845,13 +851,12 @@
         for lo, hi in row_cuts(piece, 3)
     ]
 
-    for padded, copy, raw in (
-        (ref.up_piece, coming.up_w, held.up_w),
-        (ref.down_piece, coming.down_w, held.down_w),
-    ):
-        copy.wait()
-        padded[...] = jnp.zeros((piece, ff_lanes), bf16)
-        padded[:, :units] = raw[...]
+    coming.up_w.wait()
+    coming.down_w.wait()
+    ref.up_piece[:, main:] = jnp.zeros((piece, LANES), bf16)
+    ref.up_piece[:, :units] = held.up_w[...]
+    ref.up_piece[:, units : units + rest] = held.down_w[:, main:]
+    ref.down_piece[...] = held.down_w[:, :main]
     dy_all[slot(near, kx), :] = cotangent_ref[...]
     vec_own[5:6, :] = jnp.sum(cotangent_ref[...].astype(f32), axis=0, keepdims=True)
     head_rows[...] = jnp.zeros_like(head_rows)
@@ -876,9 +881,8 @@
     share_deep(first_all, first_sems)
     for part, sems in zip(q_parts, q_sems):
         gather_finish(*part, sems)
-    down_parts[0].start(jnp.logical_or(inner, outer))
-    for part in down_parts[1:]:
-        part.start(inner)
+    for part in down_parts:
+        part.start(outer)
     gather_forward(*o_part, o_sems)
     plain_share_x(dy_all, dy_sems)
     for part in up_parts:
@@ -940,8 +944,6 @@
     part_a[half(near), :] = dot_right_t(mixed_all[half(near), :], attn_w[:, win:])
     sum_pass(0, part_a, out_sems)
     sum_near(0, part_a, out_sems)
-    for part in down_parts[1:]:
-        part.start(outer)
     for part in up_parts:
         part.second()
     up_parts[0].third()
@@ -953,6 +955,8 @@
     ref.second_hat[...] = hat
     ref.row_scale[1] = jnp.broadcast_to(inv_scale, (rows, LANES))
     second_sems = wide_share_start(second_all)
+    for part in down_parts:
+        part.start(inner)
     up_parts[1].third()
     wide_share_forward(second_all, second_sems)
     for part in down_parts:
@@ -968,13 +972,19 @@
     up_bias = shard_vector(6, stay)
     chunk = 32
 
+    in_rest = lax.broadcasted_iota(jnp.int32, (chunk, LANES), 1) < rest
+    hidden_rest = ref.hidden_rest
+
     def raise_half(side):
         part_b[half(side), :] = dot_plain(second_all[half(side), :], up_w[...])
 
         def gelu_rows(step, carry):
             at = aligned(side + step * chunk, chunk)
             value, slope = gelu_pair(part_b[at, :] + up_bias)
-            hidden_all[at, :] = value.astype(bf16)
+            last = jnp.where(in_rest, value[:, main:], 0.0)
+            hidden_all[at, :main] = value[:, :main].astype(bf16)
+            hidden_all[at, main:] = last.astype(bf16)
+            hidden_rest[at, :] = pltpu.roll(last, rest, 1).astype(bf16)
             slope_all[at, :] = slope
             return carry
 
@@ -998,7 +1008,7 @@
     down_parts[2].third()
     down_parts[0].fourth()
     plain_share_finish(dy_all, dy_sems)
-    outer_product(down_g, dy_all, hidden_all[...], 0, ff_lanes)
+    outer_product(down_g, dy_all, hidden_all[:, :main], 0, main)
     down_reduce = wide_reduce_first(down_g, ref.land_d)
     down_parts[1].fourth()
     wide_reduce_second(down_g, ref.land_d, down_reduce)
@@ -1007,24 +1017,42 @@
         part.finish()
 
     def lower_half(side):
-        part_b[half(side), :] = dot_plain(dy_all[half(side), :], down_w[...])
-
-        def slope_rows(step, total):
+        part_b[half(side), :main] = dot_plain(dy_all[half(side), :], down_w[...])
+        part_b[half(side), main:] = dot_plain(dy_all[half(side), :], up_w[:, main:])
+
+        def slope_rows(step, totals):
             at = aligned(side + step * chunk, chunk)
-            low = (part_b[at, :] * slope_all[at, :]).astype(bf16)
-            upper_all[at, :] = low
-            return total + jnp.sum(low.astype(f32), axis=0, keepdims=True)
-
-        return lax.fori_loop(0, pair // chunk, slope_rows, jnp.zeros((1, ff_lanes), f32))
+            last = pltpu.roll(part_b[at, main:], LANES - rest, 1)
+            last = jnp.where(in_rest, last * slope_all[at, main:], 0.0).astype(bf16)
+            low = (part_b[at, :main] * slope_all[at, :main]).astype(bf16)
+            upper_all[at, :main] = low
+            upper_all[at, main:] = last
+            return (
+                totals[0] + jnp.sum(low.astype(f32), axis=0, keepdims=True),
+                totals[1] + jnp.sum(last.astype(f32), axis=0, keepdims=True),
+            )
+
+        start = jnp.zeros((1, main), f32), jnp.zeros((1, LANES), f32)
+        return lax.fori_loop(0, pair // chunk, slope_rows, start)
+
+    def up_rows(step, carry):
+        at = aligned(step * tile, tile)
+        by_row = second_all[:, at]
+        up_g[at, :main] = dot_left_t(by_row, upper_all[:, :main]).astype(bf16)
+        last = dot_left_t(by_row, upper_all[:, main:])
+        last = last + dot_left_t(dy_all[:, at], hidden_rest[...])
+        up_g[at, main:] = last.astype(bf16)
+        return carry
 
     up_bias_sum = lower_half(deep)
     part_a[half(deep), :] = dot_right_t(upper_all[half(deep), :], up_w[...])
     second_sum_sems = wide_sum_deep(0, part_a)
-    up_bias_sum = up_bias_sum + lower_half(near)
-    vec_own[6:7, :] = up_bias_sum
+    more_sum = lower_half(near)
+    vec_own[6:7, :main] = up_bias_sum[0] + more_sum[0]
+    vec_own[6:7, main:] = up_bias_sum[1] + more_sum[1]
     part_a[half(near), :] = dot_right_t(upper_all[half(near), :], up_w[...])
     wide_sum_near(0, part_a, second_sum_sems)
-    outer_product(up_g, second_all, upper_all[...], 0, ff_lanes)
+    lax.fori_loop(0, D // tile, up_rows, 0)
     up_reduce = wide_reduce_first(up_g, ref.land_u)
     wide_sum_pass(0, part_a, second_sum_sems)
     wide_reduce_second(up_g, ref.land_u, up_reduce)
@@ -1041,9 +1069,14 @@
     mid_all[slot(near, c), :] = low
     vec_own[2:3, :] = jnp.sum(low.astype(f32), axis=0, keepdims=True)
     mid_sems = share_start(mid_all)
-    part_b[half(deep), :] = dot_right_t(hidden_all[half(deep), :], down_w[...])
+
+    def lower_product(side):
+        total = dot_right_t(hidden_all[half(side), :main], down_w[...])
+        return total + dot_right_t(hidden_rest[half(side), :], up_w[:, main:])
+
+    part_b[half(deep), :] = lower_product(deep)
     mlp_sems = wide_sum_deep(1, part_b)
-    part_b[half(near), :] = dot_right_t(hidden_all[half(near), :], down_w[...])
+    part_b[half(near), :] = lower_product(near)
     wide_sum_near(1, part_b, mlp_sems)
     def head_half(side_at):
         side_rows = slice(side_at * pair, (side_at + 1) * pair)
@@ -1056,13 +1089,14 @@
 
     share_forward(mid_all, mid_sems)
     share_near(mid_all, mid_sems)
-    wide_reduce_cross(down_g, ref.land_d, down_reduce)
-    wide_reduce_fourth(down_g, ref.land_d, down_reduce)
+    wide_reduce_cross(down_g, ref.land_d, down_reduce, when=outer)
+    wide_reduce_fourth(down_g, ref.land_d, down_reduce, when=outer)
     share_deep(mid_all, mid_sems)
     head_half(0)
     head_half(1)
     wide_reduce_third(up_g, ref.land_u, up_reduce)
-    wide_reduce_cross(up_g, ref.land_u, up_reduce)
+    wide_reduce_cross(down_g, ref.land_d, down_reduce, when=inner)
+    wide_reduce_fourth(down_g, ref.land_d, down_reduce, when=inner)
 
     cut = round_up(2 * width, LANES)
 
@@ -1086,8 +1120,10 @@
     lax.fori_loop(0, 2 * heads, value_back, 0, unroll=2)
     pack(qkv_grads, ref.mixed_heads, heads, 2 * width)
     lax.fori_loop(0, D // tile, value_out_rows, 0)
-    vo_args = attn_g, ref.land_vo, cut, all_lanes, net.sems(10)
+    vo_args = attn_g, ref.land_vo, cut, all_lanes, net.sems(8)
     reduce_first(*vo_args)
+
+    wide_sum_pass(1, part_b, mlp_sems)
 
     def attend_back(step, carry):
         head, span = image_head(step)
@@ -1105,10 +1141,8 @@
 
     lax.fori_loop(0, 2 * heads, attend_back, 0, unroll=2)
     pack(qkv_grads, head_rows, 2 * heads, 0)
-    wide_reduce_fourth(up_g, ref.land_u, up_reduce)
-    outer_product(attn_g, first_all, qkv_grads[:, :cut], 0, cut)
-    qk_args = attn_g, ref.land_qk, 0, cut, net.sems(10)
-    reduce_first(*qk_args, when=away)
+    wide_reduce_cross(up_g, ref.land_u, up_reduce, when=outer)
+    wide_reduce_fourth(up_g, ref.land_u, up_reduce, when=outer)
     part_a[half(deep), :] = dot_right_t(
         qkv_grads[half(deep), :qkv_lanes], attn_w[:, :qkv_lanes]
     )
@@ -1118,10 +1152,13 @@
     )
     sum_pass(1, part_a, first_sum_sems)
     sum_near(1, part_a, first_sum_sems)
-    reduce_first(*qk_args, when=home)
     vec_own[7:8, :] = jnp.sum(qkv_grads[...].astype(f32), axis=0, keepdims=True)
+    outer_product(attn_g, first_all, qkv_grads[:, :cut], 0, cut)
+    qk_args = attn_g, ref.land_qk, 0, cut, net.sems(8)
+    reduce_first(*qk_args, when=away)
     reduce_second(*vo_args)
-    wide_sum_pass(1, part_b, mlp_sems)
+    wide_reduce_cross(up_g, ref.land_u, up_reduce, when=inner)
+    wide_reduce_fourth(up_g, ref.land_u, up_reduce, when=inner)
     reduce_second(*qk_args, when=away)
     first_grad = sum_finish(1, part_a, first_sum_sems)
     back, gain_sum, shift_sum = norm_back(
@@ -1129,28 +1166,31 @@
     )
     vec_own[0:1, :] = gain_sum[None, :]
     vec_own[1:2, :] = shift_sum[None, :]
-    vec_sems = vector_planes()
+    vec_sem = vector_planes()
     ref.mid_grad[...] = ref.mid_grad[...] + back
     store(ref.mid_grad, out.input_grad)
+    reduce_first(*qk_args, when=home)
     reduce_third(*vo_args)
+    reduce_third(*qk_args, when=away)
+    vec_sem = vector_chips(vec_sem)
+    vec_sem = vector_core(vec_sem)
     reduce_second(*qk_args, when=home)
-    reduce_third(*qk_args)
-    vec_sems = vector_chips(vec_sems)
+    vector_finish(vec_sem)
+    store(ref.vec_done, out.vector_grad)
+    reduce_third(*qk_args, when=home)
     ref.down_buf[...] = wide_reduce_finish(down_g, ref.land_d, down_reduce)
     store(ref.down_buf, out.down_grad)
-    vec_sems = vector_core(vec_sems)
     mlp_rows = wide_sum_finish(1, part_b, mlp_sems)
     ref.layer_buf[...] = (ref.mid_rows[...] + mlp_rows + down_bias).astype(bf16)
     store(ref.layer_buf, out.layer_out)
-    vector_finish(vec_sems)
-    store(ref.vec_done, out.vector_grad)
     ref.up_buf[...] = wide_reduce_finish(up_g, ref.land_u, up_reduce)
     store(ref.up_buf, out.up_grad)
     ref.attn_buf[:, cut:] = reduce_finish(ref.land_vo, vo_args[4])
+    store(ref.attn_buf.at[:, cut:], out.attn_grad.at[:, cut:])
     ref.attn_buf[:, :cut] = reduce_finish(ref.land_qk, qk_args[4])
-    store(ref.attn_buf, out.attn_grad)
+    store(ref.attn_buf.at[:, :cut], out.attn_grad.at[:, :cut])
     net.drain()
-    assert net.used <= ref.send_sems.shape[0]
+    assert net.used <= ref.recv_sems.shape[0]
     for copy in stores:
         copy.wait()
 
@@ -1188,7 +1228,10 @@
     copies[3].wait()
     put_shaped(13, held[3][:, :units])
     copies[4].wait()
-    put_shaped(15, held[4][:, :units])
+    main = held[4].shape[1]
+    shaped[13][:, :main] = held[4][...]
+    shaped[13][:, main:] = held[3][:, units : 2 * units - main]
+    put(shaped[13], 15)
     copies[5].wait()
     for number, row, lo, size in (
         (2, 0, 0, D),
@@ -1237,6 +1280,8 @@
     qkv_lanes = round_up(3 * width, LANES)
     attn_lanes = round_up(4 * width, LANES)
     ff_lanes = round_up(units, LANES)
+    main = units // LANES * LANES
+    assert 2 * (units - main) <= LANES < ff_lanes - main + 1
     win = 3 * width // LANES * LANES
     given = dict(
         query_w=query_weight,
@@ -1258,32 +1303,31 @@
         down_w=down_weight.T,
     )
     place = pl.BlockSpec(memory_space=pl.ANY)
-    sem_count = 148
     cut = round_up(2 * width, LANES)
     raw_outs = dict(
         layer_out=jax.ShapeDtypeStruct((rows, D), bf16),
         input_grad=jax.ShapeDtypeStruct((rows, D), f32),
         attn_grad=jax.ShapeDtypeStruct((piece, attn_lanes), f32),
         up_grad=jax.ShapeDtypeStruct((piece, ff_lanes), f32),
-        down_grad=jax.ShapeDtypeStruct((piece, ff_lanes), f32),
+        down_grad=jax.ShapeDtypeStruct((piece, main), f32),
         vector_grad=jax.ShapeDtypeStruct((8, D), f32),
     )
     scratch = dict(
         attn_piece=pltpu.VMEM((piece, attn_lanes), bf16),
         up_piece=pltpu.VMEM((piece, ff_lanes), bf16),
-        down_piece=pltpu.VMEM((piece, ff_lanes), bf16),
+        down_piece=pltpu.VMEM((piece, main), bf16),
         up_wait=pltpu.VMEM((piece, ff_lanes), bf16),
-        down_wait=pltpu.VMEM((piece, ff_lanes), bf16),
+        down_wait=pltpu.VMEM((piece, main), bf16),
         attn_w=pltpu.VMEM((D, attn_lanes), bf16),
         up_w=pltpu.VMEM((D, ff_lanes), bf16),
-        down_w=pltpu.VMEM((D, ff_lanes), bf16),
+        down_w=pltpu.VMEM((D, main), bf16),
         attn_g=pltpu.VMEM((D, attn_lanes), bf16),
         up_g=pltpu.VMEM((D, ff_lanes), bf16),
-        down_g=pltpu.VMEM((D, ff_lanes), bf16),
+        down_g=pltpu.VMEM((D, main), bf16),
         land_vo=pltpu.VMEM((8, piece, attn_lanes - cut), bf16),
         land_qk=pltpu.VMEM((8, piece, cut), bf16),
         land_u=pltpu.VMEM((8, piece, ff_lanes), bf16),
-        land_d=pltpu.VMEM((8, piece, ff_lanes), bf16),
+        land_d=pltpu.VMEM((8, piece, main), bf16),
         first_all=pltpu.VMEM((group, D), bf16),
         second_all=pltpu.VMEM((group, D), bf16),
         dy_all=pltpu.VMEM((group, D), bf16),
@@ -1294,6 +1338,7 @@
         mixed_heads=pltpu.VMEM((heads, group, LANES), bf16),
         mixed_all=pltpu.VMEM((group, attn_lanes - win), bf16),
         hidden_all=pltpu.VMEM((group, ff_lanes), bf16),
+        hidden_rest=pltpu.VMEM((group, LANES), bf16),
         slope_all=pltpu.VMEM((group, ff_lanes), f32),
         upper_all=pltpu.VMEM((group, ff_lanes), bf16),
         qkv_grads=pltpu.VMEM((group, attn_lanes), bf16),
@@ -1322,10 +1367,10 @@
         layer_buf=pltpu.VMEM((rows, D), bf16),
         attn_buf=pltpu.VMEM((piece, attn_lanes), f32),
         up_buf=pltpu.VMEM((piece, ff_lanes), f32),
-        down_buf=pltpu.VMEM((piece, ff_lanes), f32),
-        load_sems=pltpu.SemaphoreType.DMA((len(given) + len(raw_outs),)),
-        send_sems=pltpu.SemaphoreType.DMA((sem_count,)),
-        recv_sems=pltpu.SemaphoreType.DMA((sem_count,)),
+        down_buf=pltpu.VMEM((piece, main), f32),
+        load_sems=pltpu.SemaphoreType.DMA((len(given) + len(raw_outs) + 1,)),
+        send_sems=pltpu.SemaphoreType.DMA((64,)),
+        recv_sems=pltpu.SemaphoreType.DMA((112,)),
     )
     shapes = (rows, heads, width, units, qkv_lanes, piece)
     names = tuple(given), tuple(raw_outs), tuple(scratch)

time: 162 us -> 157 us (0.969)
  Pallas kernels: 161 us -> 154 us
    pallas_call x1, Pallas kernels: 158 us -> 151 us  [fused_step(): pl.pallas_call(body, out_shape=tuple(raw_outs.values()), in_specs=[place]...]
where the time goes in v3:
time: 157 us; the launch traced here: 155 us
  Pallas kernels  154 us (98%)
    pallas_call x1, Pallas kernels, fused_step(): pl.pallas_call(body, out_shape=tuple(raw_outs.values()), in_specs=[place]...  151 us

profile of v3, /device:TPU:1, one launch (start us, length us, event | category | flops | bytes accessed | tf_op | source)
XLA Modules:
  0.0 155.2 jit_solution(12346940683625861893)
XLA Ops:
  0.7 151.2 %layer.1 = (bf16[128,1152]{1,0:T(8,128)(2,1)}, f32[128,1152]{1,0:T(8,128)}, f32[144,1152]{1,0:T(8,128)}, f32[144,1152]{1,0:T(8,128)}, f32[144,1024]{1,0:T(8,128)}, /*index=5*/f32[8,1152]{1,0:T(8,128)}) custom-call(bf16[144,288]{1,0:T(8,128)(2,1)} %refs_0_.1, bf16[144,288]{1,0:T(8,128)(2,1)} %refs_1_.1, bf16[144,288]{1,0:T(8,128)(2,1)} %refs_2_.1, ...), custom_call_target="tpu_custom_call" | custom-call | tf_op jit(solution)/shard_map/layer/pallas_call | solution.py:1381
  151.9 3.1 %outputs.1 = (bf16[128,1152]{1,0:T(8,128)(2,1)}, f32[128,1152]{1,0:T(8,128)}, f32[1152]{0:T(1024)}, f32[1152]{0:T(1024)}, f32[144,288]{1,0:T(8,128)}, /*index=5*...) custom-call(bf16[128,1152]{1,0:T(8,128)(2,1)} %get-tuple-element.40., ...), custom_call_target="tpu_custom_call" | custom-call | tf_op jit(solution)/shard_map/outputs/pallas_call | solution.py:1422

commit v4 on v3

--- a/solution.py
+++ b/solution.py
@@ -864,6 +864,144 @@
     mixed_all[...] = jnp.zeros_like(mixed_all)
     qkv_grads[...] = jnp.zeros_like(qkv_grads)
 
+    def shard_vector(row, own):
+        return jnp.where(own, vectors[row : row + 1, :], ref.far_vectors[row : row + 1, :])
+
+    scale = HD ** (-0.5)
+
+    def image_head(step):
+        head, image = lax.rem(step, heads), lax.div(step, heads)
+        return head, aligned(image * pair, pair)
+
+    def attend(step, carry):
+        head, span = image_head(step)
+        queries, keys_part = head_rows[head, span, :], head_rows[heads + head, span, :]
+        values = head_rows[2 * heads + head, span, :]
+        scores = dot_right_t(queries, keys_part) * scale
+        expo = jnp.exp(scores - jnp.max(scores, axis=1, keepdims=True))
+        probs = expo / jnp.sum(expo, axis=1, keepdims=True)
+        ref.probs_all[step] = probs
+        mixed = dot_plain(probs.astype(bf16), values)
+        ref.mixed_heads[head, span, :] = mixed.astype(bf16)
+        return carry
+
+    def pack(target, source, count, base):
+        for side_at in range(2):
+            for image in range(2):
+                at = slice(side_at * pair + image * rows, side_at * pair + (image + 1) * rows)
+                take = slice(image * pair + side_at * rows, image * pair + (side_at + 1) * rows)
+                for head in range(count):
+                    lo = base + head * HD
+                    target[at, lo : lo + HD] = source[head, take, :HD]
+
+    def half(side):
+        return aligned(side, pair)
+
+    chunk = 32
+
+    in_rest = lax.broadcasted_iota(jnp.int32, (chunk, LANES), 1) < rest
+
+    hidden_rest = ref.hidden_rest
+
+    def raise_half(side):
+        part_b[half(side), :] = dot_plain(second_all[half(side), :], up_w[...])
+
+        def gelu_rows(step, carry):
+            at = aligned(side + step * chunk, chunk)
+            value, slope = gelu_pair(part_b[at, :] + up_bias)
+            last = jnp.where(in_rest, value[:, main:], 0.0)
+            hidden_all[at, :main] = value[:, :main].astype(bf16)
+            hidden_all[at, main:] = last.astype(bf16)
+            hidden_rest[at, :] = pltpu.roll(last, rest, 1).astype(bf16)
+            slope_all[at, :] = slope
+            return carry
+
+        lax.fori_loop(0, pair // chunk, gelu_rows, 0)
+
+    tile = 3 * LANES
+
+    def outer_product(grad, left, right, lo, hi):
+        def rows_of(step, carry):
+            at = aligned(step * tile, tile)
+            grad[at, lo:hi] = dot_left_t(left[:, at], right).astype(bf16)
+            return carry
+
+        lax.fori_loop(0, D // tile, rows_of, 0, unroll=True)
+
+    def lower_half(side):
+        part_b[half(side), :main] = dot_plain(dy_all[half(side), :], down_w[...])
+        part_b[half(side), main:] = dot_plain(dy_all[half(side), :], up_w[:, main:])
+
+        def slope_rows(step, totals):
+            at = aligned(side + step * chunk, chunk)
+            last = pltpu.roll(part_b[at, main:], LANES - rest, 1)
+            last = jnp.where(in_rest, last * slope_all[at, main:], 0.0).astype(bf16)
+            low = (part_b[at, :main] * slope_all[at, :main]).astype(bf16)
+            upper_all[at, :main] = low
+            upper_all[at, main:] = last
+            return (
+                totals[0] + jnp.sum(low.astype(f32), axis=0, keepdims=True),
+                totals[1] + jnp.sum(last.astype(f32), axis=0, keepdims=True),
+            )
+
+        start = jnp.zeros((1, main), f32), jnp.zeros((1, LANES), f32)
+        return lax.fori_loop(0, pair // chunk, slope_rows, start)
+
+    def up_rows(step, carry):
+        at = aligned(step * tile, tile)
+        by_row = second_all[:, at]
+        up_g[at, :main] = dot_left_t(by_row, upper_all[:, :main]).astype(bf16)
+        last = dot_left_t(by_row, upper_all[:, main:])
+        last = last + dot_left_t(dy_all[:, at], hidden_rest[...])
+        up_g[at, main:] = last.astype(bf16)
+        return carry
+
+    def lower_product(side):
+        total = dot_right_t(hidden_all[half(side), :main], down_w[...])
+        return total + dot_right_t(hidden_rest[half(side), :], up_w[:, main:])
+
+    def head_half(side_at):
+        side_rows = slice(side_at * pair, (side_at + 1) * pair)
+        done = dot_plain(mid_all[side_rows, :], attn_w[:, win:]).astype(bf16)
+        for image in range(2):
+            to = slice(image * pair + side_at * rows, image * pair + (side_at + 1) * rows)
+            for head in range(heads):
+                lo = win_shift + head * HD
+                head_grads[head, to, :HD] = done[image * rows : (image + 1) * rows, lo : lo + HD]
+
+    cut = round_up(2 * width, LANES)
+
+    def value_back(step, carry):
+        head, span = image_head(step)
+        low = ref.probs_all[step].astype(bf16)
+        value_grad = dot_left_t(low, head_grads[head, span, :])
+        ref.mixed_heads[head, span, :] = value_grad.astype(bf16)
+        return carry
+
+    def value_out_rows(step, carry):
+        at = aligned(step * tile, tile)
+        by_value = dot_left_t(first_all[:, at], qkv_grads[:, cut:qkv_lanes])
+        by_out = dot_left_t(mid_all[:, at], mixed_all[...])
+        both = by_value[:, win - cut :] + by_out[:, :skip]
+        attn_g[at, cut:win] = by_value[:, : win - cut].astype(bf16)
+        attn_g[at, win:qkv_lanes] = both.astype(bf16)
+        attn_g[at, qkv_lanes:] = by_out[:, skip:].astype(bf16)
+        return carry
+
+    def attend_back(step, carry):
+        head, span = image_head(step)
+        queries, keys_part = head_rows[head, span, :], head_rows[heads + head, span, :]
+        values, grads = head_rows[2 * heads + head, span, :], head_grads[head, span, :]
+        probs = ref.probs_all[step]
+        prob_grad = dot_right_t(grads, values)
+        row_dot = jnp.sum(probs * prob_grad, axis=1, keepdims=True)
+        score_grad = (probs * (prob_grad - row_dot)).astype(bf16)
+        query_grad = dot_plain(score_grad, keys_part) * scale
+        key_grad = dot_left_t(score_grad, queries) * scale
+        head_rows[head, span, :] = query_grad.astype(bf16)
+        head_rows[heads + head, span, :] = key_grad.astype(bf16)
+        return carry
+
     for part in up_parts:
         part.start(inner)
     dy_sems = plain_share_z(dy_all)
@@ -879,6 +1017,8 @@
     net.arrived(ref.far_vectors, vec_sem)
     share_near(first_all, first_sems)
     share_deep(first_all, first_sems)
+    qkv_bias = shard_vector(7, home)[:, :qkv_lanes]
+    up_bias = shard_vector(6, stay)
     for part, sems in zip(q_parts, q_sems):
         gather_finish(*part, sems)
     for part in down_parts:
@@ -889,11 +1029,6 @@
         part.beside()
     for part in down_parts:
         part.beside()
-
-    def shard_vector(row, own):
-        return jnp.where(own, vectors[row : row + 1, :], ref.far_vectors[row : row + 1, :])
-
-    qkv_bias = shard_vector(7, home)[:, :qkv_lanes]
     for side_at in range(2):
         side_rows = slice(side_at * pair, (side_at + 1) * pair)
         done = dot_plain(first_all[side_rows, :], attn_w[:, :qkv_lanes])
@@ -904,48 +1039,16 @@
                 head_rows[head, to, :HD] = done[
                     image * rows : (image + 1) * rows, head * HD : (head + 1) * HD
                 ]
-    scale = HD ** (-0.5)
-
-    def image_head(step):
-        head, image = lax.rem(step, heads), lax.div(step, heads)
-        return head, aligned(image * pair, pair)
-
-    def attend(step, carry):
-        head, span = image_head(step)
-        queries, keys_part = head_rows[head, span, :], head_rows[heads + head, span, :]
-        values = head_rows[2 * heads + head, span, :]
-        scores = dot_right_t(queries, keys_part) * scale
-        expo = jnp.exp(scores - jnp.max(scores, axis=1, keepdims=True))
-        probs = expo / jnp.sum(expo, axis=1, keepdims=True)
-        ref.probs_all[step] = probs
-        mixed = dot_plain(probs.astype(bf16), values)
-        ref.mixed_heads[head, span, :] = mixed.astype(bf16)
-        return carry
-
     lax.fori_loop(0, 2 * heads, attend, 0, unroll=2)
-
-    def pack(target, source, count, base):
-        for side_at in range(2):
-            for image in range(2):
-                at = slice(side_at * pair + image * rows, side_at * pair + (image + 1) * rows)
-                take = slice(image * pair + side_at * rows, image * pair + (side_at + 1) * rows)
-                for head in range(count):
-                    lo = base + head * HD
-                    target[at, lo : lo + HD] = source[head, take, :HD]
-
     pack(mixed_all, ref.mixed_heads, heads, win_shift)
-
-    def half(side):
-        return aligned(side, pair)
-
     gather_finish(*o_part, o_sems)
     part_a[half(deep), :] = dot_right_t(mixed_all[half(deep), :], attn_w[:, win:])
     out_sems = sum_deep(0, part_a)
     part_a[half(near), :] = dot_right_t(mixed_all[half(near), :], attn_w[:, win:])
     sum_pass(0, part_a, out_sems)
     sum_near(0, part_a, out_sems)
-    for part in up_parts:
-        part.second()
+    up_parts[0].second()
+    up_parts[1].second()
     up_parts[0].third()
     attn_rows = sum_finish(0, part_a, out_sems)
     middle = tokens_ref[...].astype(f32) + attn_rows + out_bias
@@ -959,52 +1062,20 @@
         part.start(inner)
     up_parts[1].third()
     wide_share_forward(second_all, second_sems)
-    for part in down_parts:
-        part.second()
+    down_parts[0].second()
+    down_parts[1].second()
+    down_parts[2].second()
     plain_share_forward(dy_all, dy_sems)
-    for part in up_parts:
-        part.fourth()
+    up_parts[0].fourth()
+    up_parts[1].fourth()
     down_parts[0].third()
     for part in up_parts:
         part.finish()
     wide_share_near(second_all, second_sems)
-
-    up_bias = shard_vector(6, stay)
-    chunk = 32
-
-    in_rest = lax.broadcasted_iota(jnp.int32, (chunk, LANES), 1) < rest
-    hidden_rest = ref.hidden_rest
-
-    def raise_half(side):
-        part_b[half(side), :] = dot_plain(second_all[half(side), :], up_w[...])
-
-        def gelu_rows(step, carry):
-            at = aligned(side + step * chunk, chunk)
-            value, slope = gelu_pair(part_b[at, :] + up_bias)
-            last = jnp.where(in_rest, value[:, main:], 0.0)
-            hidden_all[at, :main] = value[:, :main].astype(bf16)
-            hidden_all[at, main:] = last.astype(bf16)
-            hidden_rest[at, :] = pltpu.roll(last, rest, 1).astype(bf16)
-            slope_all[at, :] = slope
-            return carry
-
-        lax.fori_loop(0, pair // chunk, gelu_rows, 0)
-
     raise_half(near)
     down_parts[1].third()
     wide_share_deep(second_all, second_sems)
     raise_half(deep)
-
-    tile = 3 * LANES
-
-    def outer_product(grad, left, right, lo, hi):
-        def rows_of(step, carry):
-            at = aligned(step * tile, tile)
-            grad[at, lo:hi] = dot_left_t(left[:, at], right).astype(bf16)
-            return carry
-
-        lax.fori_loop(0, D // tile, rows_of, 0)
-
     down_parts[2].third()
     down_parts[0].fourth()
     plain_share_finish(dy_all, dy_sems)
@@ -1015,35 +1086,6 @@
     down_parts[2].fourth()
     for part in down_parts:
         part.finish()
-
-    def lower_half(side):
-        part_b[half(side), :main] = dot_plain(dy_all[half(side), :], down_w[...])
-        part_b[half(side), main:] = dot_plain(dy_all[half(side), :], up_w[:, main:])
-
-        def slope_rows(step, totals):
-            at = aligned(side + step * chunk, chunk)
-            last = pltpu.roll(part_b[at, main:], LANES - rest, 1)
-            last = jnp.where(in_rest, last * slope_all[at, main:], 0.0).astype(bf16)
-            low = (part_b[at, :main] * slope_all[at, :main]).astype(bf16)
-            upper_all[at, :main] = low
-            upper_all[at, main:] = last
-            return (
-                totals[0] + jnp.sum(low.astype(f32), axis=0, keepdims=True),
-                totals[1] + jnp.sum(last.astype(f32), axis=0, keepdims=True),
-            )
-
-        start = jnp.zeros((1, main), f32), jnp.zeros((1, LANES), f32)
-        return lax.fori_loop(0, pair // chunk, slope_rows, start)
-
-    def up_rows(step, carry):
-        at = aligned(step * tile, tile)
-        by_row = second_all[:, at]
-        up_g[at, :main] = dot_left_t(by_row, upper_all[:, :main]).astype(bf16)
-        last = dot_left_t(by_row, upper_all[:, main:])
-        last = last + dot_left_t(dy_all[:, at], hidden_rest[...])
-        up_g[at, main:] = last.astype(bf16)
-        return carry
-
     up_bias_sum = lower_half(deep)
     part_a[half(deep), :] = dot_right_t(upper_all[half(deep), :], up_w[...])
     second_sum_sems = wide_sum_deep(0, part_a)
@@ -1052,7 +1094,7 @@
     vec_own[6:7, main:] = up_bias_sum[1] + more_sum[1]
     part_a[half(near), :] = dot_right_t(upper_all[half(near), :], up_w[...])
     wide_sum_near(0, part_a, second_sum_sems)
-    lax.fori_loop(0, D // tile, up_rows, 0)
+    lax.fori_loop(0, D // tile, up_rows, 0, unroll=True)
     up_reduce = wide_reduce_first(up_g, ref.land_u)
     wide_sum_pass(0, part_a, second_sum_sems)
     wide_reduce_second(up_g, ref.land_u, up_reduce)
@@ -1069,24 +1111,10 @@
     mid_all[slot(near, c), :] = low
     vec_own[2:3, :] = jnp.sum(low.astype(f32), axis=0, keepdims=True)
     mid_sems = share_start(mid_all)
-
-    def lower_product(side):
-        total = dot_right_t(hidden_all[half(side), :main], down_w[...])
-        return total + dot_right_t(hidden_rest[half(side), :], up_w[:, main:])
-
     part_b[half(deep), :] = lower_product(deep)
     mlp_sems = wide_sum_deep(1, part_b)
     part_b[half(near), :] = lower_product(near)
     wide_sum_near(1, part_b, mlp_sems)
-    def head_half(side_at):
-        side_rows = slice(side_at * pair, (side_at + 1) * pair)
-        done = dot_plain(mid_all[side_rows, :], attn_w[:, win:]).astype(bf16)
-        for image in range(2):
-            to = slice(image * pair + side_at * rows, image * pair + (side_at + 1) * rows)
-            for head in range(heads):
-                lo = win_shift + head * HD
-                head_grads[head, to, :HD] = done[image * rows : (image + 1) * rows, lo : lo + HD]
-
     share_forward(mid_all, mid_sems)
     share_near(mid_all, mid_sems)
     wide_reduce_cross(down_g, ref.land_d, down_reduce, when=outer)
@@ -1097,52 +1125,16 @@
     wide_reduce_third(up_g, ref.land_u, up_reduce)
     wide_reduce_cross(down_g, ref.land_d, down_reduce, when=inner)
     wide_reduce_fourth(down_g, ref.land_d, down_reduce, when=inner)
-
-    cut = round_up(2 * width, LANES)
-
-    def value_back(step, carry):
-        head, span = image_head(step)
-        low = ref.probs_all[step].astype(bf16)
-        value_grad = dot_left_t(low, head_grads[head, span, :])
-        ref.mixed_heads[head, span, :] = value_grad.astype(bf16)
-        return carry
-
-    def value_out_rows(step, carry):
-        at = aligned(step * tile, tile)
-        by_value = dot_left_t(first_all[:, at], qkv_grads[:, cut:qkv_lanes])
-        by_out = dot_left_t(mid_all[:, at], mixed_all[...])
-        both = by_value[:, win - cut :] + by_out[:, :skip]
-        attn_g[at, cut:win] = by_value[:, : win - cut].astype(bf16)
-        attn_g[at, win:qkv_lanes] = both.astype(bf16)
-        attn_g[at, qkv_lanes:] = by_out[:, skip:].astype(bf16)
-        return carry
-
     lax.fori_loop(0, 2 * heads, value_back, 0, unroll=2)
     pack(qkv_grads, ref.mixed_heads, heads, 2 * width)
     lax.fori_loop(0, D // tile, value_out_rows, 0)
     vo_args = attn_g, ref.land_vo, cut, all_lanes, net.sems(8)
     reduce_first(*vo_args)
-
     wide_sum_pass(1, part_b, mlp_sems)
-
-    def attend_back(step, carry):
-        head, span = image_head(step)
-        queries, keys_part = head_rows[head, span, :], head_rows[heads + head, span, :]
-        values, grads = head_rows[2 * heads + head, span, :], head_grads[head, span, :]
-        probs = ref.probs_all[step]
-        prob_grad = dot_right_t(grads, values)
-        row_dot = jnp.sum(probs * prob_grad, axis=1, keepdims=True)
-        score_grad = (probs * (prob_grad - row_dot)).astype(bf16)
-        query_grad = dot_plain(score_grad, keys_part) * scale
-        key_grad = dot_left_t(score_grad, queries) * scale
-        head_rows[head, span, :] = query_grad.astype(bf16)
-        head_rows[heads + head, span, :] = key_grad.astype(bf16)
-        return carry
-
     lax.fori_loop(0, 2 * heads, attend_back, 0, unroll=2)
+    wide_reduce_fourth(up_g, ref.land_u, up_reduce, when=outer)
     pack(qkv_grads, head_rows, 2 * heads, 0)
     wide_reduce_cross(up_g, ref.land_u, up_reduce, when=outer)
-    wide_reduce_fourth(up_g, ref.land_u, up_reduce, when=outer)
     part_a[half(deep), :] = dot_right_t(
         qkv_grads[half(deep), :qkv_lanes], attn_w[:, :qkv_lanes]
     )
@@ -1156,9 +1148,9 @@
     outer_product(attn_g, first_all, qkv_grads[:, :cut], 0, cut)
     qk_args = attn_g, ref.land_qk, 0, cut, net.sems(8)
     reduce_first(*qk_args, when=away)
-    reduce_second(*vo_args)
     wide_reduce_cross(up_g, ref.land_u, up_reduce, when=inner)
     wide_reduce_fourth(up_g, ref.land_u, up_reduce, when=inner)
+    reduce_second(*vo_args)
     reduce_second(*qk_args, when=away)
     first_grad = sum_finish(1, part_a, first_sum_sems)
     back, gain_sum, shift_sum = norm_back(

time: 157 us -> 155 us (0.987)
  no operation moved by 1% of the time
where the time goes in v4:
time: 155 us; the launch traced here: 154 us
  Pallas kernels  154 us (99%)
    pallas_call x1, Pallas kernels, fused_step(): pl.pallas_call(body, out_shape=tuple(raw_outs.values()), in_specs=[place]...  150 us
    pallas_call x1, Pallas kernels, fused_step(): pl.pallas_call(format_body, out_shape=outs, in_specs=[place] * 6, out_spe...  3.11 us

profile of v4, /device:TPU:1, one launch (start us, length us, event | category | flops | bytes accessed | tf_op | source)
XLA Modules:
  0.0 154.4 jit_solution(2099037126469667111)
XLA Ops:
  0.7 150.5 %layer.1 = (bf16[128,1152]{1,0:T(8,128)(2,1)}, f32[128,1152]{1,0:T(8,128)}, f32[144,1152]{1,0:T(8,128)}, f32[144,1152]{1,0:T(8,128)}, f32[144,1024]{1,0:T(8,128)}, /*index=5*/f32[8,1152]{1,0:T(8,128)}) custom-call(bf16[144,288]{1,0:T(8,128)(2,1)} %refs_0_.1, bf16[144,288]{1,0:T(8,128)(2,1)} %refs_1_.1, bf16[144,288]{1,0:T(8,128)(2,1)} %refs_2_.1, ...), custom_call_target="tpu_custom_call" | custom-call | tf_op jit(solution)/shard_map/layer/pallas_call | solution.py:1373
  151.1 3.1 %outputs.1 = (bf16[128,1152]{1,0:T(8,128)(2,1)}, f32[128,1152]{1,0:T(8,128)}, f32[1152]{0:T(1024)}, f32[1152]{0:T(1024)}, f32[144,288]{1,0:T(8,128)}, /*index=5*...) custom-call(bf16[128,1152]{1,0:T(8,128)(2,1)} %get-tuple-element.40., ...), custom_call_target="tpu_custom_call" | custom-call | tf_op jit(solution)/shard_map/outputs/pallas_call | solution.py:1414

commit v5 on v4

--- a/solution.py
+++ b/solution.py
@@ -844,7 +844,7 @@
     net.send(vectors, ref.far_vectors, dev_far, vec_sem)
     up_parts = [
         WideGather(ref.up_piece, up_w, ref.up_wait, lo, hi)
-        for lo, hi in row_cuts(piece, 2)
+        for lo, hi in ((0, 64), (64, 144))
     ]
     down_parts = [
         WideGather(ref.down_piece, down_w, ref.down_wait, lo, hi)
@@ -1039,7 +1039,7 @@
                 head_rows[head, to, :HD] = done[
                     image * rows : (image + 1) * rows, head * HD : (head + 1) * HD
                 ]
-    lax.fori_loop(0, 2 * heads, attend, 0, unroll=2)
+    lax.fori_loop(0, 2 * heads, attend, 0, unroll=4)
     pack(mixed_all, ref.mixed_heads, heads, win_shift)
     gather_finish(*o_part, o_sems)
     part_a[half(deep), :] = dot_right_t(mixed_all[half(deep), :], attn_w[:, win:])
@@ -1116,8 +1116,8 @@
     part_b[half(near), :] = lower_product(near)
     wide_sum_near(1, part_b, mlp_sems)
     share_forward(mid_all, mid_sems)
+    wide_reduce_cross(down_g, ref.land_d, down_reduce, when=outer)
     share_near(mid_all, mid_sems)
-    wide_reduce_cross(down_g, ref.land_d, down_reduce, when=outer)
     wide_reduce_fourth(down_g, ref.land_d, down_reduce, when=outer)
     share_deep(mid_all, mid_sems)
     head_half(0)
@@ -1148,9 +1148,9 @@
     outer_product(attn_g, first_all, qkv_grads[:, :cut], 0, cut)
     qk_args = attn_g, ref.land_qk, 0, cut, net.sems(8)
     reduce_first(*qk_args, when=away)
-    wide_reduce_cross(up_g, ref.land_u, up_reduce, when=inner)
     wide_reduce_fourth(up_g, ref.land_u, up_reduce, when=inner)
     reduce_second(*vo_args)
+    wide_reduce_cross(up_g, ref.land_u, up_reduce, when=inner)
     reduce_second(*qk_args, when=away)
     first_grad = sum_finish(1, part_a, first_sum_sems)
     back, gain_sum, shift_sum = norm_back(

time: 155 us -> 154 us (level)
  no operation moved by 1% of the time
where the time goes in v5:
time: 154 us
  Pallas kernels  153 us (99%)
    pallas_call x1, Pallas kernels, fused_step(): pl.pallas_call(body, out_shape=tuple(raw_outs.values()), in_specs=[place]...  150 us
    pallas_call x1, Pallas kernels, fused_step(): pl.pallas_call(format_body, out_shape=outs, in_specs=[place] * 6, out_spe...  3.11 us

profile of v5, /device:TPU:1, one launch (start us, length us, event | category | flops | bytes accessed | tf_op | source)
XLA Modules:
  0.0 153.9 jit_solution(8339253082890375587)
XLA Ops:
  0.7 150.0 %layer.1 = (bf16[128,1152]{1,0:T(8,128)(2,1)}, f32[128,1152]{1,0:T(8,128)}, f32[144,1152]{1,0:T(8,128)}, f32[144,1152]{1,0:T(8,128)}, f32[144,1024]{1,0:T(8,128)}, /*index=5*/f32[8,1152]{1,0:T(8,128)}) custom-call(bf16[144,288]{1,0:T(8,128)(2,1)} %refs_0_.1, bf16[144,288]{1,0:T(8,128)(2,1)} %refs_1_.1, bf16[144,288]{1,0:T(8,128)(2,1)} %refs_2_.1, ...), custom_call_target="tpu_custom_call" | custom-call | tf_op jit(solution)/shard_map/layer/pallas_call | solution.py:1373
  150.6 3.1 %outputs.1 = (bf16[128,1152]{1,0:T(8,128)(2,1)}, f32[128,1152]{1,0:T(8,128)}, f32[1152]{0:T(1024)}, f32[1152]{0:T(1024)}, f32[144,288]{1,0:T(8,128)}, /*index=5*...) custom-call(bf16[128,1152]{1,0:T(8,128)(2,1)} %get-tuple-element.40., ...), custom_call_target="tpu_custom_call" | custom-call | tf_op jit(solution)/shard_map/outputs/pallas_call | solution.py:1414

commit v6 on v5

--- a/solution.py
+++ b/solution.py
@@ -1361,8 +1361,8 @@
         up_buf=pltpu.VMEM((piece, ff_lanes), f32),
         down_buf=pltpu.VMEM((piece, main), f32),
         load_sems=pltpu.SemaphoreType.DMA((len(given) + len(raw_outs) + 1,)),
-        send_sems=pltpu.SemaphoreType.DMA((64,)),
-        recv_sems=pltpu.SemaphoreType.DMA((112,)),
+        send_sems=pltpu.SemaphoreType.DMA((48,)),
+        recv_sems=pltpu.SemaphoreType.DMA((108,)),
     )
     shapes = (rows, heads, width, units, qkv_lanes, piece)
     names = tuple(given), tuple(raw_outs), tuple(scratch)

time: 154 us -> 154 us (level)
  no operation moved by 1% of the time
where the time goes in v6:
time: 154 us
  Pallas kernels  153 us (99%)
    pallas_call x1, Pallas kernels, fused_step(): pl.pallas_call(body, out_shape=tuple(raw_outs.values()), in_specs=[place]...  150 us
    pallas_call x1, Pallas kernels, fused_step(): pl.pallas_call(format_body, out_shape=outs, in_specs=[place] * 6, out_spe...  3.11 us

profile of v6, /device:TPU:1, one launch (start us, length us, event | category | flops | bytes accessed | tf_op | source)
XLA Modules:
  0.0 153.7 jit_solution(3210419011600815790)
XLA Ops:
  0.7 149.8 %layer.1 = (bf16[128,1152]{1,0:T(8,128)(2,1)}, f32[128,1152]{1,0:T(8,128)}, f32[144,1152]{1,0:T(8,128)}, f32[144,1152]{1,0:T(8,128)}, f32[144,1024]{1,0:T(8,128)}, /*index=5*/f32[8,1152]{1,0:T(8,128)}) custom-call(bf16[144,288]{1,0:T(8,128)(2,1)} %refs_0_.1, bf16[144,288]{1,0:T(8,128)(2,1)} %refs_1_.1, bf16[144,288]{1,0:T(8,128)(2,1)} %refs_2_.1, ...), custom_call_target="tpu_custom_call" | custom-call | tf_op jit(solution)/shard_map/layer/pallas_call | solution.py:1373
  150.5 3.1 %outputs.1 = (bf16[128,1152]{1,0:T(8,128)(2,1)}, f32[128,1152]{1,0:T(8,128)}, f32[1152]{0:T(1024)}, f32[1152]{0:T(1024)}, f32[144,288]{1,0:T(8,128)}, /*index=5*...) custom-call(bf16[128,1152]{1,0:T(8,128)(2,1)} %get-tuple-element.40., ...), custom_call_target="tpu_custom_call" | custom-call | tf_op jit(solution)/shard_map/outputs/pallas_call | solution.py:1414
